TPU v7x, 512 devices: a whole 4x8x8 slice. The times are simulated.
512 devices in a mesh: ctx: 128 (over y, z, core), tp: 4 (over x).
Axes of the slice: x: 4, y: 8, z: 8, core: 2. Of those that a mesh axis runs over, the one named last changes fastest.
Arguments:
- streams: bfloat16 [3, 8192, 16384], P(None, 'tp', 'ctx'), may hold values from -6 to 6
- short_weight: float32 [3, 3, 8192], P(None, None, 'tp')
- filters: float32 [512, 16384], P('tp', 'ctx'), may hold values from -0.046875 to 0.046875
- skip_gain: float32 [8192], P('tp'), may hold values from -4 to 4
- norm_gain: float32 [8192], P('tp'), may hold values from 0.5 to 1.5
Outputs:
- block_out: bfloat16 [8192, 16384], P('tp', 'ctx')
All inputs are finite; a program needn't handle non-finite values.
Results may differ from a plain program's by a relative error of at most 0.0064.
Values may be sent and summed in bfloat16 or wider, within the bound.
No kernel may reach another device: no remote copies, remote signals or barrier semaphores. Data moves between devices by JAX's collectives and lax.ppermute only.
A program may use at most 64 MiB of HBM per device.

v0:
```python
import jax
import jax.numpy as jnp
from jax import lax
from jax.experimental import pallas as pl
from jax.experimental.pallas import tpu as pltpu
from jax.sharding import PartitionSpec as P

bf16 = jnp.bfloat16
f32 = jnp.float32
LANES = 128
SLOT = 24


def long_conv_blocks(recv, owned):
    blocks = recv.shape[0]
    half = blocks // 2
    rows = half * owned
    span = 2
    wide = 2 * LANES

    def kernel(recv_ref, out_ref, toep_ref, cols_ref, acc_ref):
        even = recv_ref[:, 0, 0:owned, :].reshape(rows, LANES)
        odd = recv_ref[:, 1, 0:owned, :].reshape(rows, LANES)
        for lag in range(span):
            skip = lag * owned
            if lag:
                cols_ref[0:skip, lag * wide : (lag + 1) * wide] = jnp.zeros((skip, wide), bf16)
            cols_ref[skip:rows, lag * wide : lag * wide + LANES] = even[0 : rows - skip]
            cols_ref[skip:rows, lag * wide + LANES : (lag + 1) * wide] = odd[0 : rows - skip]
        acc_ref[...] = jnp.zeros_like(acc_ref)
        upper = lax.broadcasted_iota(jnp.int32, (LANES, LANES), 1) >= lax.broadcasted_iota(
            jnp.int32, (LANES, LANES), 0
        )
        toep_ref[0] = jnp.zeros((LANES, LANES), bf16)

        def build(first, count, before):
            for k in range(first, first + count):
                taps = recv_ref[k // 2, k % 2, owned : owned + 8, :].astype(f32)[0:1]
                turned = pltpu.roll(jnp.broadcast_to(taps, (LANES, LANES)), 0, 1, stride=1, stride_axis=0)
                toep_ref[k + 1] = jnp.where(upper, turned, before).astype(bf16)
                before = turned
            return before

        before = build(0, 2 * span, jnp.zeros((LANES, LANES), f32))
        for step in range(half // span):
            if (step + 1) * span < half:
                before = build((step + 1) * 2 * span, 2 * span, before)
            parts = []
            for lag in range(step * span, (step + 1) * span):
                parts.append(jnp.concatenate([toep_ref[2 * lag + 1], toep_ref[2 * lag + 2]], axis=1))
                parts.append(jnp.concatenate([toep_ref[2 * lag], toep_ref[2 * lag + 1]], axis=1))
            start = step * span * owned
            acc_ref[start:rows, :] += jnp.dot(
                cols_ref[0 : rows - start, :], jnp.concatenate(parts, axis=0), preferred_element_type=f32
            )
        out_ref[:, 0] = acc_ref[:, 0:LANES].astype(bf16).reshape(half, owned, LANES)
        out_ref[:, 1] = acc_ref[:, LANES:wide].astype(bf16).reshape(half, owned, LANES)

    out = pl.pallas_call(
        kernel,
        out_shape=jax.ShapeDtypeStruct((half, 2, owned, LANES), bf16),
        in_specs=[pl.BlockSpec(memory_space=pltpu.VMEM)],
        out_specs=pl.BlockSpec(memory_space=pltpu.VMEM),
        scratch_shapes=[
            pltpu.VMEM((blocks + 1, LANES, LANES), bf16),
            pltpu.VMEM((rows, span * wide), bf16),
            pltpu.VMEM((rows, wide), f32),
        ],
        compiler_params=pltpu.CompilerParams(vmem_limit_bytes=32 << 20),
        name="long_conv",
    )(recv.reshape(half, 2, recv.shape[1], LANES))
    return out.reshape(blocks, owned, LANES)


def shards(streams, short_weight, filters, skip_gain, norm_gain):
    n_ctx = lax.axis_size("ctx")
    n_width = lax.axis_size("tp")
    tok_rows = streams.shape[2]
    local_chan = streams.shape[1]
    owned = local_chan // n_ctx
    taps = short_weight.shape[0]
    tail = lax.ppermute(streams[:, :, tok_rows - (taps - 1) :], "ctx", [(i, i + 1) for i in range(n_ctx - 1)])
    padded = jnp.concatenate([tail, streams], axis=2).astype(f32)
    conv = jnp.zeros(streams.shape, f32)
    for offset in range(taps):
        start = taps - 1 - offset
        conv = conv + short_weight[offset][:, :, None] * padded[:, :, start : start + tok_rows]
    query = lax.optimization_barrier(conv[0].astype(bf16))
    product = lax.optimization_barrier((conv[1] * conv[2]).astype(bf16))
    send = jnp.concatenate(
        [
            product.reshape(n_ctx, owned, tok_rows),
            filters.astype(bf16)[:, None, :],
            jnp.zeros((n_ctx, SLOT - owned - 1, tok_rows), bf16),
        ],
        axis=1,
    )
    recv = lax.all_to_all(send, "ctx", 0, 0)
    mixed = long_conv_blocks(recv, owned)
    back = lax.all_to_all(mixed, "ctx", 0, 0).reshape(local_chan, tok_rows)
    gated = (
        query.astype(f32) * (back.astype(f32) + skip_gain[:, None] * product.astype(f32))
    ).astype(bf16)
    gated_wide = lax.optimization_barrier(gated).astype(f32)
    squares = lax.psum(jnp.sum(gated_wide * gated_wide, axis=0), "tp")
    rms = jnp.sqrt(squares / (local_chan * n_width) + 1e-05)
    return (gated_wide * norm_gain[:, None] / rms[None, :]).astype(bf16)


def solution(mesh):
    in_specs = (P(None, "tp", "ctx"), P(None, None, "tp"), P("tp", "ctx"), P("tp"), P("tp"))
    out_specs = P("tp", "ctx")
    return jax.shard_map(shards, mesh=mesh, in_specs=in_specs, out_specs=out_specs, check_vma=False)
```

profile of v0, /device:TPU:8, one launch (start us, length us, event | category | flops | bytes accessed | tf_op | source)
XLA Modules:
  0.0 106.5 jit_solution(5765873672452581027)
XLA Ops:
  0.0 0.0 copy-start
  0.0 0.0 copy-start.2
  0.0 0.0 copy-start.3
  0.0 2.0 %slice.32 = bf16[3,2048,2]{2,1,0:T(8,128)(2,1)S(1)} slice(bf16[3,2048,128]{2,1,0:T(8,128)(2,1)} %param.5), slice={[0:3], [0:2048], [126:128]} | slice | bytes 49152 | tf_op jit(solution)/shard_map/slice | solution.py:82
  2.0 0.7 copy.10
  2.8 1.9 %collective-permute-start = (bf16[3,2048,2]{1,2,0:T(2,128)(2,1)S(1)}, bf16[3,2048,2]{1,2,0:T(2,128)(2,1)S(1)}, u32[]{:S(2)}, u32[]{:S(2)}) collective-permute-start(bf16[3,2048,2]{1,2,0:T(2,128)(2,1)S(1)} %copy.10), channel_id=1, source_target_pairs={{0,4},{4,8},{8,12},{12,16},{16,20},{20,24},{24,28},{28,32},{32,36}... | collective-permute-start | bytes 73736 | tf_op jit(solution)/shard_map/ppermute | solution.py:82
  4.7 0.0 copy-done.2
  4.7 0.0 copy-done.3
  4.7 0.1 copy.9
  4.8 0.1 pad.2.clone
  4.9 9.6 %collective-permute-done = bf16[3,2048,2]{1,2,0:T(2,128)(2,1)S(1)} collective-permute-done((bf16[3,2048,2]{1,2,0:T(2,128)(2,1)S(1)}, bf16[3,2048,2]{1,2,0:T(2,128)(2,1)S(1)}, u32[]{:S(2)}, u32[]{:S(2)}) %collective-permute-start) | collective-permute-done | bytes 24608 | tf_op jit(solution)/shard_map/ppermute | solution.py:82
  14.5 0.9 copy.8
  15.4 0.0 copy-done
  15.4 1.1 %maximum_convert_fusion = f32[3,2048,130]{2,1,0:T(8,128)S(1)} fusion(bf16[3,2048,128]{2,1,0:T(8,128)(2,1)S(1)} %copy-done, bf16[3,2048,2]{2,1,0:T(8,128)(2,1)S(1)} %copy.8), kind=kLoop, calls=%fused_computation.5 | loop fusion | flops 3194880 | bytes 4792320 | tf_op jit(solution)/shard_map/convert_element_type | solution.py:83
  16.5 4.7 %fusion = f32[3,2048,128]{2,1,0:T(8,128)S(1)} fusion(f32[3,2048,130]{2,1,0:T(8,128)S(1)} %maximum_convert_fusion, f32[3,2048]{1,0:T(4,128)S(1)} %get-tuple-element.6, f32[3,2048]{1,0:T(4,128)S(1)} %get-tuple-element.7, f32[3,2048]{1,0:T(4,128)S(1)} %get-tuple-element.5), kind=kLoop, calls=%fused_computation.1 | loop fusion | flops 3932160 | bytes 12656640 | tf_op jit(solution)/shard_map/add | solution.py:87
  21.2 0.1 fusion.9
  21.3 0.0 copy-start.1
  21.4 0.8 copy-done.1
  22.1 0.0 copy-start.4
  22.1 0.2 maximum_maximum_fusion
  22.4 37.6 %all_to_all.10 = bf16[128,24,128]{2,1,0:T(8,128)(2,1)S(1)} all-to-all(bf16[128,24,128]{2,1,0:T(8,128)(2,1)S(1)} %maximum_maximum_fusion), channel_id=1, replica_groups=mesh['ctx'=128,'tp'=4] {'ctx'}, dimensions={0} | all-to-all | bytes 1572864 | tf_op jit(solution)/shard_map/all_to_all | solution.py:98
  60.0 0.0 copy-start.5
  60.0 5.7 %long_conv.1 = bf16[64,2,16,128]{3,2,1,0:T(8,128)(2,1)} custom-call(bf16[64,2,24,128]{3,2,1,0:T(8,128)(2,1)S(1)} %bitcast.18), custom_call_target="tpu_custom_call" | custom-call | tf_op jit(solution)/shard_map/long_conv/pallas_call | solution.py:59
  65.6 7.2 %all-to-all-start.1 = ((bf16[128,16,128]{2,1,0:T(8,128)(2,1)}), bf16[128,16,128]{2,1,0:T(8,128)(2,1)}, u32[]{:S(2)}, u32[]{:S(2)}) async-start(bf16[128,16,128]{2,1,0:T(8,128)(2,1)} %bitcast.8), calls=%async_computation.1 | async-start | bytes 1048576 | tf_op jit(solution)/shard_map/all_to_all | solution.py:100
  72.9 0.8 fusion.8
  73.7 19.1 %all-to-all-done.1 = bf16[128,16,128]{2,1,0:T(8,128)(2,1)} async-done(((bf16[128,16,128]{2,1,0:T(8,128)(2,1)}), bf16[128,16,128]{2,1,0:T(8,128)(2,1)}, u32[]{:S(2)}, u32[]{:S(2)}) %all-to-all-start.1) | async-done | bytes 524320 | tf_op jit(solution)/shard_map/all_to_all | solution.py:100
  92.8 0.0 copy-done.4
  92.8 1.7 %fusion.7 = bf16[2048,128]{1,0:T(8,128)(2,1)S(1)} fusion(bf16[2048,128]{1,0:T(8,128)(2,1)} %copy-done.1, bf16[2048,128]{1,0:T(8,128)(2,1)} %fusion.8, bf16[128,16,128]{2,1,0:T(8,128)(2,1)} %all-to-all-done.1, f32[2048]{0:T(1024)S(1)} %copy-done.4), kind=kLoop, calls=%fused_computation.16 | loop fusion | flops 1835008 | bytes 2105344 | tf_op jit(solution)/shard_map/convert_element_type | solution.py:103
  94.6 0.3 fusion.4
  94.8 10.5 %psum.7 = f32[128]{0:T(128)S(1)} all-reduce(f32[128]{0:T(128)S(1)} %fusion.4), channel_id=1, replica_groups=mesh['ctx'=128,'tp'=4] {'tp'}, use_global_device_ids=true, to_apply=%region_1.0 | all-reduce | flops 128 | bytes 1024 | tf_op jit(solution)/shard_map/psum | solution.py:105
  105.3 0.0 copy-done.5
  105.3 1.1 %fusion.3 = bf16[2048,128]{1,0:T(8,128)(2,1)} fusion(bf16[2048,128]{1,0:T(8,128)(2,1)S(1)} %fusion.7, f32[128]{0:T(128)S(1)} %add_sqrt_fusion, f32[2048]{0:T(1024)S(1)} %copy-done.5), kind=kLoop, calls=%fused_computation.9 | loop fusion | flops 1048576 | bytes 1057280 | tf_op jit(solution)/shard_map/convert_element_type | solution.py:107
  (4 shorter events, 0.0 us)
Async XLA Ops:
  0.0 15.4 %copy-start = (bf16[3,2048,128]{2,1,0:T(8,128)(2,1)S(1)}, bf16[3,2048,128]{2,1,0:T(8,128)(2,1)}, u32[]{:S(2)}) copy-start(bf16[3,2048,128]{2,1,0:T(8,128)(2,1)} %param.5) | copy-start | bytes 4718596
  0.0 4.7 %copy-start.2 = (f32[3,3,2048]{2,1,0:T(4,128)S(1)}, f32[3,3,2048]{2,1,0:T(4,128)}, u32[]{:S(2)}) copy-start(f32[3,3,2048]{2,1,0:T(4,128)} %param.6) | copy-start | bytes 221188
  0.0 4.7 %copy-start.3 = (f32[128,128]{1,0:T(8,128)S(1)}, f32[128,128]{1,0:T(8,128)}, u32[]{:S(2)}) copy-start(f32[128,128]{1,0:T(8,128)} %param.7) | copy-start | bytes 196612
  2.8 11.8 %collective-permute-start = (bf16[3,2048,2]{1,2,0:T(2,128)(2,1)S(1)}, bf16[3,2048,2]{1,2,0:T(2,128)(2,1)S(1)}, u32[]{:S(2)}, u32[]{:S(2)}) collective-permute-start(bf16[3,2048,2]{1,2,0:T(2,128)(2,1)S(1)} %copy.10), channel_id=1, source_target_pairs={{0,4},{4,8},{8,12},{12,16},{16,20},{20,24},{24,28},{28,32},{32,36}... | collective-permute-start | bytes 73736 | tf_op jit(solution)/shard_map/ppermute | solution.py:82
  21.3 0.8 copy-start.1
  22.1 70.7 %copy-start.4 = (f32[2048]{0:T(1024)S(1)}, f32[2048]{0:T(1024)}, u32[]{:S(2)}) copy-start(f32[2048]{0:T(1024)} %param.8) | copy-start | bytes 24580
  60.0 45.4 %copy-start.5 = (f32[2048]{0:T(1024)S(1)}, f32[2048]{0:T(1024)}, u32[]{:S(2)}) copy-start(f32[2048]{0:T(1024)} %param.9) | copy-start | bytes 24580
  65.6 27.2 %all-to-all-start.1 = ((bf16[128,16,128]{2,1,0:T(8,128)(2,1)}), bf16[128,16,128]{2,1,0:T(8,128)(2,1)}, u32[]{:S(2)}, u32[]{:S(2)}) async-start(bf16[128,16,128]{2,1,0:T(8,128)(2,1)} %bitcast.8), calls=%async_computation.1 | async-start | bytes 1048576 | tf_op jit(solution)/shard_map/all_to_all | solution.py:100
where the time goes:
time: 107 us; the launch traced here: 106 us
  blocking collectives  48.1 us (45%)
  waiting for transfers between devices  28.8 us (27%)
  other arithmetic  9.29 us (9%)
  starting transfers between devices  9.16 us (9%)
  Pallas kernels  5.66 us (5%)
  local copies, waits for them, and re-layouts  5.41 us (5%)
    all_to_all x1, blocking collectives, shards(): recv = lax.all_to_all(send, 'ctx', 0, 0)  37.6 us
    all_to_all x1, waiting for transfers between devices, shards(): back = lax.all_to_all(mixed, 'ctx', 0, 0).reshape(local_chan, tok_rows)  19.1 us
    psum x1, blocking collectives, shards(): squares = lax.psum(jnp.sum(gated_wide * gated_wide, axis=0), 'tp')  10.5 us
    ppermute x1, waiting for transfers between devices, shards(): lax.ppermute(streams[:, :, tok_rows - (taps - 1):], 'ctx', [(i, i + 1) fo...  9.64 us
    all_to_all x1, starting transfers between devices, shards(): back = lax.all_to_all(mixed, 'ctx', 0, 0).reshape(local_chan, tok_rows)  7.24 us
    pallas_call x1, Pallas kernels, long_conv_blocks(): pl.pallas_call(kernel, out_shape=jax.ShapeDtypeStruct((half, 2, owned, LA...  5.66 us
    add x1, other arithmetic, shards(): conv + short_weight[offset][:, :, None] * padded[:, :, start:start + tok_...  4.67 us
  transfers between devices with their start and end apart: 2, of which 2 were waited for; matrix products, arithmetic and copies ran while one was open for 1% of the time, Pallas kernels for 0%

commit v1 on v0

v1 whole, which is shorter than its diff:
```python
import jax
import jax.numpy as jnp
import numpy as np
from jax import lax
from jax.experimental import pallas as pl
from jax.experimental.pallas import tpu as pltpu
from jax.sharding import PartitionSpec as P

bf16 = jnp.bfloat16
f32 = jnp.float32
LANES = 128
SLOT = 24


def lane_iota(shape):
    return lax.broadcasted_iota(jnp.int32, shape, len(shape) - 1)


def row_iota(shape):
    return lax.broadcasted_iota(jnp.int32, shape, len(shape) - 2)


ENDS = (0, 1, LANES - 2, LANES - 1)


def pack_product(streams, short_weight, filters, owned):
    chan = streams.shape[1]
    owners = chan // owned
    chunk = 256
    taps = short_weight.shape[0]

    def kernel(key_ref, value_ref, weight_ref, filt_ref, out_ref, ends_ref):
        src = row_iota((LANES, LANES))
        dst = lane_iota((LANES, LANES))
        shifts = jnp.concatenate(
            [jnp.where(dst == src + j, 1.0, 0.0) for j in range(1, taps)], axis=1
        ).astype(bf16)
        place = dst // owned
        pick = []
        for stream in range(2):
            hit = jnp.zeros((LANES, LANES), f32)
            for n, pos in enumerate(ENDS):
                hit = jnp.where((place == 4 * stream + n) & (src == pos), 1.0, hit)
            pick.append(hit)
        pick = jnp.concatenate(pick, axis=0).astype(bf16)
        shape = (chunk, LANES)
        inner = lane_iota(shape) >= taps - 1
        same = lane_iota(shape) % owned == row_iota(shape) % owned
        ends = jnp.zeros((owners, LANES), f32)
        for first in range(0, chan, chunk):
            rows = slice(first, first + chunk)
            columns = jnp.transpose(weight_ref[:, rows])
            key = key_ref[0, rows, :]
            value = value_ref[0, rows, :]
            convs = []
            for stream, raw in ((1, key), (2, value)):
                moved = jnp.dot(raw, shifts, preferred_element_type=f32)
                total = columns[:, stream : stream + 1] * raw.astype(f32)
                for j in range(1, taps):
                    total = total + columns[:, 3 * j + stream : 3 * j + stream + 1] * (
                        moved[:, (j - 1) * LANES : j * LANES]
                    )
                convs.append(total)
            product = jnp.where(inner, convs[0] * convs[1], 0.0).astype(bf16)
            out_ref[first // owned : (first + chunk) // owned, 0:owned, :] = product.reshape(
                chunk // owned, owned, LANES
            )
            spread = jnp.dot(jnp.concatenate([key, value], axis=1), pick, preferred_element_type=f32)
            spread = jnp.where(same, spread, 0.0).astype(bf16)
            group_shape = (owners, chunk)
            member = row_iota(group_shape) == (lane_iota(group_shape) + first) // owned
            ends = ends + jnp.dot(
                jnp.where(member, 1.0, 0.0).astype(bf16), spread, preferred_element_type=f32
            )
        ends_ref[...] = ends
        sub = row_iota((8, LANES))
        for owner in range(owners):
            row = jnp.where(
                sub == 0,
                jnp.broadcast_to(filt_ref[owner : owner + 1, :], (8, LANES)),
                jnp.broadcast_to(ends_ref[owner : owner + 1, :], (8, LANES)),
            )
            out_ref[owner, owned : owned + 8, :] = jnp.where(sub < 2, row, 0.0).astype(bf16)

    weights = jnp.pad(short_weight.reshape(3 * taps, chan), ((0, 16 - 3 * taps), (0, 0)))
    return pl.pallas_call(
        kernel,
        grid=(1,),
        out_shape=jax.ShapeDtypeStruct((owners, SLOT, LANES), bf16),
        in_specs=[
            pl.BlockSpec((1, chan, LANES), lambda i: (1, 0, 0)),
            pl.BlockSpec((1, chan, LANES), lambda i: (2, 0, 0)),
            pl.BlockSpec((16, chan), lambda i: (0, 0)),
            pl.BlockSpec((owners, LANES), lambda i: (0, 0)),
        ],
        out_specs=pl.BlockSpec((owners, SLOT, LANES), lambda i: (0, 0, 0)),
        scratch_shapes=[pltpu.VMEM((owners, LANES), f32)],
        compiler_params=pltpu.CompilerParams(vmem_limit_bytes=32 << 20),
        name="pack_product",
    )(streams, streams, weights, filters)


def end_terms(owned):
    pick = np.zeros((2 * LANES, 6 * LANES), np.float32)
    for stream in range(2):
        base = 4 * stream
        for n, sources in enumerate((((0, 0), (1, 0)), ((3, 1), (0, 0)), ((2, 1), (3, 1)))):
            for pos, (end, before) in enumerate(sources):
                for c in range(owned):
                    row = before * LANES + (base + end) * owned + c
                    pick[row, (3 * stream + n) * LANES + pos * owned + c] = 1.0
    return jnp.asarray(pick, bf16)


def long_conv_blocks(recv, own_weight, owned):
    blocks = recv.shape[0]
    half = blocks // 2
    rows = half * owned
    span = 2
    wide = 2 * LANES
    chunk = 256

    def kernel(recv_ref, weight_ref, terms_ref, out_ref, toep_ref, cols_ref, acc_ref, ends_ref, first_ref):
        for k in range(blocks):
            ends_ref[k : k + 1, :] = recv_ref[k // 2, k % 2, owned : owned + 8, :].astype(f32)[1:2]
        ends = ends_ref[...]
        before = jnp.where(row_iota(ends.shape) == 0, 0.0, pltpu.roll(ends, 1, 0))
        both = jnp.concatenate([ends, before], axis=1).astype(bf16)
        terms = jnp.dot(both, terms_ref[...], preferred_element_type=f32)
        convs = []
        for stream in range(2):
            total = jnp.zeros((blocks, LANES), f32)
            for n in range(3):
                at = 3 * stream + n
                total = total + weight_ref[at : at + 1, :] * terms[:, at * LANES : (at + 1) * LANES]
            convs.append(total)
        first_ref[...] = (convs[0] * convs[1]).astype(bf16)
        shape = (chunk, LANES)
        same = lane_iota(shape) % owned == row_iota(shape) % owned
        src = row_iota((LANES, LANES))
        dst = lane_iota((LANES, LANES))
        to_lane = jnp.where((src // owned == dst) & (dst < 2), 1.0, 0.0).astype(bf16)
        for lag in range(1, span):
            cols_ref[0 : lag * owned, lag * wide : (lag + 1) * wide] = jnp.zeros((lag * owned, wide), bf16)
        for parity in range(2):
            for begin in range(0, rows, chunk):
                block = 2 * ((row_iota(shape) + begin) // owned) + parity
                member = jnp.where(lane_iota(shape) == block, 1.0, 0.0).astype(bf16)
                spread = jnp.dot(member, first_ref[...], preferred_element_type=f32)
                spread = jnp.where(same, spread, 0.0).astype(bf16)
                patch = jnp.dot(spread, to_lane, preferred_element_type=f32)
                part = recv_ref[begin // owned : (begin + chunk) // owned, parity, 0:owned, :]
                part = (part.reshape(chunk, LANES).astype(f32) + patch).astype(bf16)
                for lag in range(span):
                    top = begin + lag * owned
                    size = min(chunk, rows - top)
                    left = lag * wide + parity * LANES
                    cols_ref[top : top + size, left : left + LANES] = part[0:size]
        acc_ref[...] = jnp.zeros_like(acc_ref)
        upper = dst >= src
        toep_ref[0] = jnp.zeros((LANES, LANES), bf16)

        def build(first, count, before):
            for k in range(first, first + count):
                taps = recv_ref[k // 2, k % 2, owned : owned + 8, :].astype(f32)[0:1]
                turned = pltpu.roll(jnp.broadcast_to(taps, (LANES, LANES)), 0, 1, stride=1, stride_axis=0)
                toep_ref[k + 1] = jnp.where(upper, turned, before).astype(bf16)
                before = turned
            return before

        before = build(0, 2 * span, jnp.zeros((LANES, LANES), f32))
        for step in range(half // span):
            if (step + 1) * span < half:
                before = build((step + 1) * 2 * span, 2 * span, before)
            parts = []
            for lag in range(step * span, (step + 1) * span):
                parts.append(jnp.concatenate([toep_ref[2 * lag + 1], toep_ref[2 * lag + 2]], axis=1))
                parts.append(jnp.concatenate([toep_ref[2 * lag], toep_ref[2 * lag + 1]], axis=1))
            start = step * span * owned
            acc_ref[start:rows, :] += jnp.dot(
                cols_ref[0 : rows - start, :], jnp.concatenate(parts, axis=0), preferred_element_type=f32
            )
        out_ref[:, 0] = acc_ref[:, 0:LANES].astype(bf16).reshape(half, owned, LANES)
        out_ref[:, 1] = acc_ref[:, LANES:wide].astype(bf16).reshape(half, owned, LANES)

    vmem = pl.BlockSpec(memory_space=pltpu.VMEM)
    out = pl.pallas_call(
        kernel,
        out_shape=jax.ShapeDtypeStruct((half, 2, owned, LANES), bf16),
        in_specs=[vmem, vmem, vmem],
        out_specs=vmem,
        scratch_shapes=[
            pltpu.VMEM((blocks + 1, LANES, LANES), bf16),
            pltpu.VMEM((rows, span * wide), bf16),
            pltpu.VMEM((rows, wide), f32),
            pltpu.VMEM((blocks, LANES), f32),
            pltpu.VMEM((blocks, LANES), bf16),
        ],
        compiler_params=pltpu.CompilerParams(vmem_limit_bytes=32 << 20),
        name="long_conv",
    )(recv.reshape(half, 2, recv.shape[1], LANES), own_weight, end_terms(owned))
    return out.reshape(blocks, owned, LANES)


def local_streams(streams, short_weight, n_ctx):
    taps = short_weight.shape[0]
    length = streams.shape[2]
    tail = lax.ppermute(streams[:, :, length - (taps - 1) :], "ctx", [(i, i + 1) for i in range(n_ctx - 1)])
    padded = jnp.concatenate([tail, streams], axis=2).astype(f32)
    conv = jnp.zeros(streams.shape, f32)
    for offset in range(taps):
        start = taps - 1 - offset
        conv = conv + short_weight[offset][:, :, None] * padded[:, :, start : start + length]
    return lax.optimization_barrier((conv[0].astype(bf16), (conv[1] * conv[2]).astype(bf16)))


def shards(streams, short_weight, filters, skip_gain, norm_gain):
    n_ctx = lax.axis_size("ctx")
    n_width = lax.axis_size("tp")
    length = streams.shape[2]
    local_chan = streams.shape[1]
    owned = local_chan // n_ctx
    taps = short_weight.shape[0]
    send = pack_product(streams, short_weight, filters, owned)
    recv = lax.all_to_all(send, "ctx", 0, 0)
    streams, short_weight, skip_gain, norm_gain, _ = lax.optimization_barrier(
        (streams, short_weight, skip_gain, norm_gain, send)
    )
    own_weight = lax.dynamic_slice_in_dim(short_weight, lax.axis_index("ctx") * owned, owned, 2)
    own_weight = jnp.transpose(own_weight[:, 1:], (1, 0, 2)).reshape(2 * taps, owned)
    own_weight = jnp.pad(jnp.tile(own_weight, (1, 2)), ((0, 8 - 2 * taps), (0, LANES - 2 * owned)))
    query, product = local_streams(streams, short_weight, n_ctx)
    direct = skip_gain[:, None] * product.astype(f32)
    gain = jnp.broadcast_to(norm_gain[:, None], (local_chan, length))
    direct, gain, own_weight, query, recv = lax.optimization_barrier((direct, gain, own_weight, query, recv))
    mixed = long_conv_blocks(recv, own_weight, owned)
    back = lax.all_to_all(mixed, "ctx", 0, 0).reshape(local_chan, length)
    gated = (query.astype(f32) * (back.astype(f32) + direct)).astype(bf16)
    gated_wide = lax.optimization_barrier(gated).astype(f32)
    squares = jnp.sum(lax.all_gather(jnp.sum(gated_wide * gated_wide, axis=0), "tp"), axis=0)
    rms = jnp.sqrt(squares / (local_chan * n_width) + 1e-05)
    return (gated_wide * gain / rms[None, :]).astype(bf16)


def solution(mesh):
    in_specs = (P(None, "tp", "ctx"), P(None, None, "tp"), P("tp", "ctx"), P("tp"), P("tp"))
    out_specs = P("tp", "ctx")
    return jax.shard_map(shards, mesh=mesh, in_specs=in_specs, out_specs=out_specs, check_vma=False)
```

time: 107 us -> 104 us (0.972)
  waiting for transfers between devices: 28.8 us -> 13.1 us
  starting transfers between devices: 9.16 us -> 19.6 us
  blocking collectives: 48.1 us -> 43 us
  Pallas kernels: 5.66 us -> 8.86 us
  local copies, waits for them, and re-layouts: 5.41 us -> 8.44 us
    all_to_all x1, waiting for transfers between devices: 19.1 us -> 0.01 us  [shards(): recv = lax.all_to_all(send, 'ctx', 0, 0)]
    psum x1 -> x0, blocking collectives: 10.5 us -> none  [shards(): squares = lax.psum(jnp.sum(gated_wide * gated_wide, axis=0), 'tp')]
    all_to_all x1, starting transfers between devices: 7.24 us -> 17.5 us  [shards(): recv = lax.all_to_all(send, 'ctx', 0, 0)]
    all_gather x0 -> x1, blocking collectives: none -> 9.66 us  [shards(): lax.all_gather(jnp.sum(gated_wide * gated_wide, axis=0), 'tp')]
    all_to_all x1, blocking collectives: 37.6 us -> 33.4 us  [shards(): back = lax.all_to_all(mixed, 'ctx', 0, 0).reshape(local_chan, length)]
    ppermute x1, waiting for transfers between devices: 9.64 us -> 13.1 us  [local_streams(): lax.ppermute(streams[:, :, length - (taps - 1):], 'ctx', [(i, i + 1) for...]
    pallas_call x0 -> x1, Pallas kernels: none -> 3.29 us  [pack_product(): pl.pallas_call(kernel, grid=(1,), out_shape=jax.ShapeDtypeStruct((owners,...]
    optimization_barrier x0 -> x1, local copies, waits for them, and re-layouts: none -> 1.65 us  [shards(): lax.optimization_barrier((streams, short_weight, skip_gain, norm_gain, se...]
  transfers between devices with their start and end apart: 2 -> 2, of which waited for: 2 -> 1; matrix products, arithmetic and copies ran while one was open for 1% -> 13% of each run, Pallas kernels for 0% -> 0%
where the time goes in v1:
time: 104 us; the launch traced here: 103 us
  blocking collectives  43 us (41%)
  starting transfers between devices  19.6 us (19%)
  waiting for transfers between devices  13.1 us (13%)
  other arithmetic  10.1 us (10%)
  Pallas kernels  8.86 us (9%)
  local copies, waits for them, and re-layouts  8.44 us (8%)
    all_to_all x1, blocking collectives, shards(): back = lax.all_to_all(mixed, 'ctx', 0, 0).reshape(local_chan, length)  33.4 us
    all_to_all x1, starting transfers between devices, shards(): recv = lax.all_to_all(send, 'ctx', 0, 0)  17.5 us
    ppermute x1, waiting for transfers between devices, local_streams(): lax.ppermute(streams[:, :, length - (taps - 1):], 'ctx', [(i, i + 1) for...  13.1 us
    all_gather x1, blocking collectives, shards(): lax.all_gather(jnp.sum(gated_wide * gated_wide, axis=0), 'tp')  9.66 us
    pallas_call x1, Pallas kernels, long_conv_blocks(): pl.pallas_call(kernel, out_shape=jax.ShapeDtypeStruct((half, 2, owned, LA...  5.57 us
    add x1, other arithmetic, local_streams(): conv + short_weight[offset][:, :, None] * padded[:, :, start:start + length]  4.67 us
    pallas_call x1, Pallas kernels, pack_product(): pl.pallas_call(kernel, grid=(1,), out_shape=jax.ShapeDtypeStruct((owners,...  3.29 us
    unnamed x16, local copies, waits for them, and re-layouts  2.76 us
  transfers between devices with their start and end apart: 2, of which 1 were waited for; matrix products, arithmetic and copies ran while one was open for 13% of the time, Pallas kernels for 0%

profile of v1, /device:TPU:8, one launch (start us, length us, event | category | flops | bytes accessed | tf_op | source)
XLA Modules:
  0.0 103.2 jit_solution(3421649203281064558)
XLA Ops:
  0.0 0.9 reshape.29
  1.0 0.0 copy-start
  1.0 1.4 %copy-done = bf16[3,2048,128]{2,1,0:T(8,128)(2,1)S(1)} copy-done((bf16[3,2048,128]{2,1,0:T(8,128)(2,1)S(1)}, bf16[3,2048,128]{2,1,0:T(8,128)(2,1)}, u32[]{:S(2)}) %copy-start) | copy-done | bytes 1572888
  2.4 0.8 copy-done.3
  3.2 3.3 %pack_product.1 = bf16[128,24,128]{2,1,0:T(8,128)(2,1)} custom-call(bf16[3,2048,128]{2,1,0:T(8,128)(2,1)S(1)} %copy-done, bf16[3,2048,128]{2,1,0:T(8,128)(2,1)S(1)} %copy-done, f32[16,2048]{1,0:T(8,128)S(1)} %pad.8.weight_ref, f32[128,128]{1,0:T(8,128)S(1)} %copy-done.3), custom_call_target="tpu_custom_call" | custom-call | tf_op jit(solution)/shard_map/pack_product/pallas_call | solution.py:86
  6.5 17.5 %all-to-all-start = ((bf16[128,24,128]{2,1,0:T(8,128)(2,1)}), bf16[128,24,128]{2,1,0:T(8,128)(2,1)S(1)}, u32[]{:S(2)}, u32[]{:S(2)}) async-start(bf16[128,24,128]{2,1,0:T(8,128)(2,1)} %pack_product.1), calls=%async_computation | async-start | bytes 1572864 | tf_op jit(solution)/shard_map/all_to_all | solution.py:225
  24.0 1.7 %copy.9 = bf16[3,2048,128]{1,2,0:T(8,128)(2,1)} copy(bf16[3,2048,128]{2,1,0:T(8,128)(2,1)S(1)} %copy-done.1) | data formatting | bytes 3145728 | tf_op jit(solution)/shard_map/optimization_barrier | solution.py:226
  25.7 0.9 slice.45
  26.6 2.1 %collective-permute-start = (bf16[3,2048,2]{1,2,0:T(2,128)(2,1)S(1)}, bf16[3,2048,2]{1,2,0:T(2,128)(2,1)S(1)}, u32[]{:S(2)}, u32[]{:S(2)}) collective-permute-start(bf16[3,2048,2]{1,2,0:T(2,128)(2,1)S(1)} %slice.45), channel_id=1, source_target_pairs={{0,4},{4,8},{8,12},{12,16},{16,20},{20,24},{24,28},{28,32},{32,36}... | collective-permute-start | bytes 73736 | tf_op jit(solution)/shard_map/ppermute | solution.py:208
  28.7 0.1 dynamic-slice_bitcast_fusion
  28.8 0.1 tile.12
  28.9 13.1 %collective-permute-done = bf16[3,2048,2]{1,2,0:T(2,128)(2,1)S(1)} collective-permute-done((bf16[3,2048,2]{1,2,0:T(2,128)(2,1)S(1)}, bf16[3,2048,2]{1,2,0:T(2,128)(2,1)S(1)}, u32[]{:S(2)}, u32[]{:S(2)}) %collective-permute-start) | collective-permute-done | bytes 24608 | tf_op jit(solution)/shard_map/ppermute | solution.py:208
  42.0 1.6 %copy.10 = bf16[3,2048,2]{2,1,0:T(8,128)(2,1)} copy(bf16[3,2048,2]{1,2,0:T(2,128)(2,1)S(1)} %collective-permute-done) | data formatting | bytes 49152 | tf_op jit(solution)/shard_map/ppermute | solution.py:208
  43.6 2.5 %maximum_convert_fusion = f32[3,2048,130]{2,1,0:T(8,128)S(1)} fusion(bf16[3,2048,128]{2,1,0:T(8,128)(2,1)S(1)} %copy-done.1, bf16[3,2048,2]{2,1,0:T(8,128)(2,1)} %copy.10), kind=kLoop, calls=%fused_computation.5 | loop fusion | flops 3194880 | bytes 4792320 | tf_op jit(solution)/shard_map/convert_element_type | solution.py:209
  46.1 4.7 %fusion = f32[3,2048,128]{2,1,0:T(8,128)S(1)} fusion(f32[3,2048,130]{2,1,0:T(8,128)S(1)} %maximum_convert_fusion, f32[3,2048]{1,0:T(4,128)S(1)} %get-tuple-element.28, f32[3,2048]{1,0:T(4,128)S(1)} %get-tuple-element.29, f32[3,2048]{1,0:T(4,128)S(1)} %get-tuple-element.27), kind=kLoop, calls=%fused_computation.1 | loop fusion | flops 3932160 | bytes 12656640 | tf_op jit(solution)/shard_map/add | solution.py:213
  50.8 0.0 copy-start.6
  50.8 0.0 copy-start.7
  50.8 0.0 copy-start.2
  50.8 0.1 fusion.8
  50.9 0.1 fusion.9
  51.0 0.5 copy-done.6
  51.5 1.3 %convert_multiply_fusion.2 = f32[2048,128]{1,0:T(8,128)} fusion(bf16[2048,128]{1,0:T(8,128)(2,1)S(1)} %fusion.9, f32[2048]{0:T(1024)S(1)} %copy-done.6), kind=kLoop, calls=%fused_computation.17 | loop fusion | flops 524288 | bytes 1581056 | tf_op jit(solution)/shard_map/mul | solution.py:233
  52.8 0.0 all-to-all-done
  52.8 0.0 copy-done.7
  52.8 0.3 broadcast_in_dim.2
  53.2 5.6 %long_conv.1 = bf16[64,2,16,128]{3,2,1,0:T(8,128)(2,1)S(1)} custom-call(bf16[64,2,24,128]{3,2,1,0:T(8,128)(2,1)S(1)} %bitcast.18, f32[8,128]{1,0:T(8,128)S(1)} %pad.9.weight_ref, bf16[256,768]{1,0:T(8,128)(2,1)S(1)} %copy-done.2), custom_call_target="tpu_custom_call" | custom-call | tf_op jit(solution)/shard_map/long_conv/pallas_call | solution.py:187
  58.7 33.4 %all_to_all.10 = bf16[128,16,128]{2,1,0:T(8,128)(2,1)S(1)} all-to-all(bf16[128,16,128]{2,1,0:T(8,128)(2,1)S(1)} %bitcast.19), channel_id=1, replica_groups=mesh['ctx'=128,'tp'=4] {'ctx'}, dimensions={0} | all-to-all | bytes 1048576 | tf_op jit(solution)/shard_map/all_to_all | solution.py:237
  92.1 0.0 copy-done.4
  92.1 0.2 fusion.7
  92.3 0.3 fusion.4
  92.6 9.7 %all-gather.1 = f32[4,1,128]{2,1,0:T(1,128)S(1)} all-gather(f32[1,1,128]{2,1,0:T(1,128)S(1)} %bitcast.20), channel_id=2, replica_groups=mesh['ctx'=128,'tp'=4] {'tp'}, dimensions={0}, use_global_device_ids=true | all-gather | bytes 2560 | tf_op jit(solution)/shard_map/all_gather | solution.py:240
  102.3 0.9 fusion.3
  (15 shorter events, 0.1 us)
Async XLA Ops:
  1.0 1.4 %copy-start = (bf16[3,2048,128]{2,1,0:T(8,128)(2,1)S(1)}, bf16[3,2048,128]{2,1,0:T(8,128)(2,1)}, u32[]{:S(2)}) copy-start(bf16[3,2048,128]{2,1,0:T(8,128)(2,1)} %value_ref.1) | copy-start | bytes 4718596
  2.4 0.8 copy-start.3
  3.2 20.8 %copy-start.1 = (bf16[3,2048,128]{2,1,0:T(8,128)(2,1)S(1)}, bf16[3,2048,128]{2,1,0:T(8,128)(2,1)}, u32[]{:S(2)}) copy-start(bf16[3,2048,128]{2,1,0:T(8,128)(2,1)} %value_ref.1) | copy-start | bytes 4718596
  6.5 22.2 %copy-start.5 = (f32[3,3,2048]{2,1,0:T(4,128)S(1)}, f32[3,3,2048]{2,1,0:T(4,128)}, u32[]{:S(2)}) copy-start(f32[3,3,2048]{2,1,0:T(4,128)} %param.7) | copy-start | bytes 221188
  6.5 46.3 %all-to-all-start = ((bf16[128,24,128]{2,1,0:T(8,128)(2,1)}), bf16[128,24,128]{2,1,0:T(8,128)(2,1)S(1)}, u32[]{:S(2)}, u32[]{:S(2)}) async-start(bf16[128,24,128]{2,1,0:T(8,128)(2,1)} %pack_product.1), calls=%async_computation | async-start | bytes 1572864 | tf_op jit(solution)/shard_map/all_to_all | solution.py:225
  26.6 15.4 %collective-permute-start = (bf16[3,2048,2]{1,2,0:T(2,128)(2,1)S(1)}, bf16[3,2048,2]{1,2,0:T(2,128)(2,1)S(1)}, u32[]{:S(2)}, u32[]{:S(2)}) collective-permute-start(bf16[3,2048,2]{1,2,0:T(2,128)(2,1)S(1)} %slice.45), channel_id=1, source_target_pairs={{0,4},{4,8},{8,12},{12,16},{16,20},{20,24},{24,28},{28,32},{32,36}... | collective-permute-start | bytes 73736 | tf_op jit(solution)/shard_map/ppermute | solution.py:208
  50.8 0.7 copy-start.6
  50.8 2.0 %copy-start.7 = (f32[2048]{0:T(1024)S(1)}, f32[2048]{0:T(1024)}, u32[]{:S(2)}) copy-start(f32[2048]{0:T(1024)} %param.10) | copy-start | bytes 24580
  50.8 2.3 %copy-start.2 = (bf16[256,768]{1,0:T(8,128)(2,1)S(1)}, bf16[256,768]{1,0:T(8,128)(2,1)}, u32[]{:S(2)}) copy-start(bf16[256,768]{1,0:T(8,128)(2,1)} %constant.22.clone.terms_ref) | copy-start | bytes 1179652
  52.8 39.3 %copy-start.4 = (f32[2048,128]{1,0:T(8,128)S(1)}, f32[2048,128]{1,0:T(8,128)}, u32[]{:S(2)}) copy-start(f32[2048,128]{1,0:T(8,128)} %convert_multiply_fusion.2) | copy-start | bytes 3145732

commit v2 on v1

--- a/solution.py
+++ b/solution.py
@@ -202,10 +202,9 @@
     return out.reshape(blocks, owned, LANES)
 
 
-def local_streams(streams, short_weight, n_ctx):
+def local_streams(streams, tail, short_weight):
     taps = short_weight.shape[0]
     length = streams.shape[2]
-    tail = lax.ppermute(streams[:, :, length - (taps - 1) :], "ctx", [(i, i + 1) for i in range(n_ctx - 1)])
     padded = jnp.concatenate([tail, streams], axis=2).astype(f32)
     conv = jnp.zeros(streams.shape, f32)
     for offset in range(taps):
@@ -223,18 +222,20 @@
     taps = short_weight.shape[0]
     send = pack_product(streams, short_weight, filters, owned)
     recv = lax.all_to_all(send, "ctx", 0, 0)
-    streams, short_weight, skip_gain, norm_gain, _ = lax.optimization_barrier(
-        (streams, short_weight, skip_gain, norm_gain, send)
-    )
+    streams, short_weight, _ = lax.optimization_barrier((streams, short_weight, send))
     own_weight = lax.dynamic_slice_in_dim(short_weight, lax.axis_index("ctx") * owned, owned, 2)
     own_weight = jnp.transpose(own_weight[:, 1:], (1, 0, 2)).reshape(2 * taps, owned)
     own_weight = jnp.pad(jnp.tile(own_weight, (1, 2)), ((0, 8 - 2 * taps), (0, LANES - 2 * owned)))
-    query, product = local_streams(streams, short_weight, n_ctx)
+    tail = lax.ppermute(streams[:, :, length - (taps - 1) :], "ctx", [(i, i + 1) for i in range(n_ctx - 1)])
+    mixed = long_conv_blocks(recv, own_weight, owned)
+    back = lax.all_to_all(mixed, "ctx", 0, 0).reshape(local_chan, length)
+    streams, tail, short_weight, skip_gain, norm_gain, _ = lax.optimization_barrier(
+        (streams, tail, short_weight, skip_gain, norm_gain, mixed)
+    )
+    query, product = local_streams(streams, tail, short_weight)
     direct = skip_gain[:, None] * product.astype(f32)
     gain = jnp.broadcast_to(norm_gain[:, None], (local_chan, length))
-    direct, gain, own_weight, query, recv = lax.optimization_barrier((direct, gain, own_weight, query, recv))
-    mixed = long_conv_blocks(recv, own_weight, owned)
-    back = lax.all_to_all(mixed, "ctx", 0, 0).reshape(local_chan, length)
+    direct, gain, query, back = lax.optimization_barrier((direct, gain, query, back))
     gated = (query.astype(f32) * (back.astype(f32) + direct)).astype(bf16)
     gated_wide = lax.optimization_barrier(gated).astype(f32)
     squares = jnp.sum(lax.all_gather(jnp.sum(gated_wide * gated_wide, axis=0), "tp"), axis=0)

time: 104 us -> 96.4 us (0.927)
  blocking collectives: 43 us -> 9.66 us
  waiting for transfers between devices: 13.1 us -> 33.2 us
  starting transfers between devices: 19.6 us -> 26.8 us
  other arithmetic: 10.1 us -> 8.71 us
    all_to_all x1 -> x0, blocking collectives: 33.4 us -> none  [shards(): back = lax.all_to_all(mixed, 'ctx', 0, 0).reshape(local_chan, length)]
    all_to_all x1, waiting for transfers between devices: 0.01 us -> 21.1 us  [shards(): recv = lax.all_to_all(send, 'ctx', 0, 0)]
    ppermute x1, waiting for transfers between devices: 13.1 us -> 0.01 us  [shards(): lax.ppermute(streams[:, :, length - (taps - 1):], 'ctx', [(i, i + 1) for...]
    all_to_all x0 -> x1, waiting for transfers between devices: none -> 12.2 us  [shards(): back = lax.all_to_all(mixed, 'ctx', 0, 0).reshape(local_chan, length)]
    all_to_all x0 -> x1, starting transfers between devices: none -> 7.25 us  [shards(): back = lax.all_to_all(mixed, 'ctx', 0, 0).reshape(local_chan, length)]
    ppermute x1 -> x0, local copies, waits for them, and re-layouts: 1.58 us -> none  [local_streams(): lax.ppermute(streams[:, :, length - (taps - 1):], 'ctx', [(i, i + 1) for...]
    convert_element_type x1, other arithmetic: 2.53 us -> 1.13 us  [local_streams(): padded = jnp.concatenate([tail, streams], axis=2).astype(f32)]
    optimization_barrier x1 -> x2, local copies, waits for them, and re-layouts: 1.65 us -> 2.47 us  [the longest x1 1.59 us: shards(): lax.optimization_barrier((streams, short_weight, send))]
  transfers between devices with their start and end apart: 2 -> 3, of which waited for: 1 -> 2; matrix products, arithmetic and copies ran while one was open for 13% -> 10% of each run, Pallas kernels for 0% -> 7%
where the time goes in v2:
time: 96.4 us; the launch traced here: 95.9 us
  waiting for transfers between devices  33.2 us (34%)
  starting transfers between devices  26.8 us (28%)
  blocking collectives  9.66 us (10%)
  Pallas kernels  9.64 us (10%)
  other arithmetic  8.71 us (9%)
  local copies, waits for them, and re-layouts  7.68 us (8%)
    all_to_all x1, waiting for transfers between devices, shards(): recv = lax.all_to_all(send, 'ctx', 0, 0)  21.1 us
    all_to_all x1, starting transfers between devices, shards(): recv = lax.all_to_all(send, 'ctx', 0, 0)  17.5 us
    all_to_all x1, waiting for transfers between devices, shards(): back = lax.all_to_all(mixed, 'ctx', 0, 0).reshape(local_chan, length)  12.2 us
    all_gather x1, blocking collectives, shards(): lax.all_gather(jnp.sum(gated_wide * gated_wide, axis=0), 'tp')  9.66 us
    all_to_all x1, starting transfers between devices, shards(): back = lax.all_to_all(mixed, 'ctx', 0, 0).reshape(local_chan, length)  7.25 us
    pallas_call x1, Pallas kernels, long_conv_blocks(): pl.pallas_call(kernel, out_shape=jax.ShapeDtypeStruct((half, 2, owned, LA...  6.36 us
    add x1, other arithmetic, local_streams(): conv + short_weight[offset][:, :, None] * padded[:, :, start:start + length]  4.67 us
    pallas_call x1, Pallas kernels, pack_product(): pl.pallas_call(kernel, grid=(1,), out_shape=jax.ShapeDtypeStruct((owners,...  3.28 us
  transfers between devices with their start and end apart: 3, of which 2 were waited for; matrix products, arithmetic and copies ran while one was open for 10% of the time, Pallas kernels for 7%

profile of v2, /device:TPU:8, one launch (start us, length us, event | category | flops | bytes accessed | tf_op | source)
XLA Modules:
  0.0 95.9 jit_solution(11454545945857180260)
XLA Ops:
  0.0 0.9 reshape.29
  1.0 0.0 copy-start
  1.0 1.4 %copy-done = bf16[3,2048,128]{2,1,0:T(8,128)(2,1)S(1)} copy-done((bf16[3,2048,128]{2,1,0:T(8,128)(2,1)S(1)}, bf16[3,2048,128]{2,1,0:T(8,128)(2,1)}, u32[]{:S(2)}) %copy-start) | copy-done | bytes 1572888
  2.4 0.8 copy-done.3
  3.2 3.3 %pack_product.1 = bf16[128,24,128]{2,1,0:T(8,128)(2,1)} custom-call(bf16[3,2048,128]{2,1,0:T(8,128)(2,1)S(1)} %copy-done, bf16[3,2048,128]{2,1,0:T(8,128)(2,1)S(1)} %copy-done, f32[16,2048]{1,0:T(8,128)S(1)} %pad.8.weight_ref, f32[128,128]{1,0:T(8,128)S(1)} %copy-done.3), custom_call_target="tpu_custom_call" | custom-call | tf_op jit(solution)/shard_map/pack_product/pallas_call | solution.py:86
  6.5 17.5 %all-to-all-start = ((bf16[128,24,128]{2,1,0:T(8,128)(2,1)}), bf16[128,24,128]{2,1,0:T(8,128)(2,1)S(1)}, u32[]{:S(2)}, u32[]{:S(2)}) async-start(bf16[128,24,128]{2,1,0:T(8,128)(2,1)} %pack_product.1), calls=%async_computation | async-start | bytes 1572864 | tf_op jit(solution)/shard_map/all_to_all | solution.py:224
  24.0 0.0 copy-done.1
  24.0 1.6 %copy.9 = bf16[3,2048,128]{1,2,0:T(8,128)(2,1)} copy(bf16[3,2048,128]{2,1,0:T(8,128)(2,1)S(1)} %copy-done.1) | data formatting | bytes 3145728 | tf_op jit(solution)/shard_map/optimization_barrier | solution.py:225
  25.6 0.9 slice.45
  26.5 2.1 %collective-permute-start = (bf16[3,2048,2]{1,2,0:T(2,128)(2,1)S(1)}, bf16[3,2048,2]{1,2,0:T(2,128)(2,1)S(1)}, u32[]{:S(2)}, u32[]{:S(2)}) collective-permute-start(bf16[3,2048,2]{1,2,0:T(2,128)(2,1)S(1)} %slice.45), channel_id=1, source_target_pairs={{0,4},{4,8},{8,12},{12,16},{16,20},{20,24},{24,28},{28,32},{32,36}... | collective-permute-start | bytes 73736 | tf_op jit(solution)/shard_map/ppermute | solution.py:229
  28.6 0.0 copy-done.4
  28.6 0.1 dynamic-slice_bitcast_fusion
  28.7 0.1 tile.12
  28.8 21.1 %all-to-all-done = bf16[128,24,128]{2,1,0:T(8,128)(2,1)S(1)} async-done(((bf16[128,24,128]{2,1,0:T(8,128)(2,1)}), bf16[128,24,128]{2,1,0:T(8,128)(2,1)S(1)}, u32[]{:S(2)}, u32[]{:S(2)}) %all-to-all-start) | async-done | bytes 786464 | tf_op jit(solution)/shard_map/all_to_all | solution.py:224
  49.9 6.4 %long_conv.1 = bf16[64,2,16,128]{3,2,1,0:T(8,128)(2,1)} custom-call(bf16[64,2,24,128]{3,2,1,0:T(8,128)(2,1)S(1)} %bitcast.16, f32[8,128]{1,0:T(8,128)S(1)} %pad.9.weight_ref, bf16[256,768]{1,0:T(8,128)(2,1)S(1)} %copy-done.2), custom_call_target="tpu_custom_call" | custom-call | tf_op jit(solution)/shard_map/long_conv/pallas_call | solution.py:187
  56.2 7.3 %all-to-all-start.1 = ((bf16[128,16,128]{2,1,0:T(8,128)(2,1)}), bf16[128,16,128]{2,1,0:T(8,128)(2,1)}, u32[]{:S(2)}, u32[]{:S(2)}) async-start(bf16[128,16,128]{2,1,0:T(8,128)(2,1)} %bitcast.2), calls=%async_computation.1 | async-start | bytes 1048576 | tf_op jit(solution)/shard_map/all_to_all | solution.py:231
  63.5 0.0 collective-permute-done
  63.5 0.9 copy.11
  64.4 1.1 %maximum_convert_fusion = f32[3,2048,130]{2,1,0:T(8,128)S(1)} fusion(bf16[3,2048,128]{2,1,0:T(8,128)(2,1)S(1)} %copy-done.1, bf16[3,2048,2]{2,1,0:T(8,128)(2,1)S(1)} %copy.11), kind=kLoop, calls=%fused_computation.5 | loop fusion | flops 3194880 | bytes 4792320 | tf_op jit(solution)/shard_map/convert_element_type | solution.py:208
  65.6 4.7 %fusion = f32[3,2048,128]{2,1,0:T(8,128)S(1)} fusion(f32[3,2048,130]{2,1,0:T(8,128)S(1)} %maximum_convert_fusion, f32[3,2048]{1,0:T(4,128)S(1)} %get-tuple-element.32, f32[3,2048]{1,0:T(4,128)S(1)} %get-tuple-element.33, f32[3,2048]{1,0:T(4,128)S(1)} %get-tuple-element.31), kind=kLoop, calls=%fused_computation.1 | loop fusion | flops 3932160 | bytes 12656640 | tf_op jit(solution)/shard_map/add | solution.py:212
  70.2 0.0 copy-start.5
  70.2 0.0 copy-start.6
  70.3 0.1 fusion.6
  70.3 0.1 fusion.7
  70.4 0.5 copy-done.5
  70.9 0.3 convert_multiply_fusion.2
  71.3 12.2 %all-to-all-done.1 = bf16[128,16,128]{2,1,0:T(8,128)(2,1)} async-done(((bf16[128,16,128]{2,1,0:T(8,128)(2,1)}), bf16[128,16,128]{2,1,0:T(8,128)(2,1)}, u32[]{:S(2)}, u32[]{:S(2)}) %all-to-all-start.1) | async-done | bytes 524320 | tf_op jit(solution)/shard_map/all_to_all | solution.py:231
  83.5 0.3 broadcast_in_dim.2
  83.8 1.2 %multiply_convert_fusion = bf16[2048,128]{1,0:T(8,128)(2,1)S(1)} fusion(f32[2048,128]{1,0:T(8,128)S(1)} %convert_multiply_fusion.2, bf16[2048,128]{1,0:T(8,128)(2,1)} %bitcast.8, bf16[2048,128]{1,0:T(8,128)(2,1)S(1)} %fusion.6), kind=kLoop, calls=%fused_computation.14 | loop fusion | flops 1310720 | bytes 2621440 | tf_op jit(solution)/shard_map/convert_element_type | solution.py:239
  85.0 0.3 fusion.4
  85.3 9.7 %all-gather.1 = f32[4,1,128]{2,1,0:T(1,128)S(1)} all-gather(f32[1,1,128]{2,1,0:T(1,128)S(1)} %bitcast.17), channel_id=2, replica_groups=mesh['ctx'=128,'tp'=4] {'tp'}, dimensions={0}, use_global_device_ids=true | all-gather | bytes 2560 | tf_op jit(solution)/shard_map/all_gather | solution.py:241
  95.0 0.9 fusion.3
  (14 shorter events, 0.1 us)
Async XLA Ops:
  1.0 1.4 %copy-start = (bf16[3,2048,128]{2,1,0:T(8,128)(2,1)S(1)}, bf16[3,2048,128]{2,1,0:T(8,128)(2,1)}, u32[]{:S(2)}) copy-start(bf16[3,2048,128]{2,1,0:T(8,128)(2,1)} %value_ref.1) | copy-start | bytes 4718596
  2.4 0.8 copy-start.3
  3.2 20.8 %copy-start.1 = (bf16[3,2048,128]{2,1,0:T(8,128)(2,1)S(1)}, bf16[3,2048,128]{2,1,0:T(8,128)(2,1)}, u32[]{:S(2)}) copy-start(bf16[3,2048,128]{2,1,0:T(8,128)(2,1)} %value_ref.1) | copy-start | bytes 4718596
  6.5 22.1 %copy-start.4 = (f32[3,3,2048]{2,1,0:T(4,128)S(1)}, f32[3,3,2048]{2,1,0:T(4,128)}, u32[]{:S(2)}) copy-start(f32[3,3,2048]{2,1,0:T(4,128)} %param.7) | copy-start | bytes 221188
  6.5 43.4 %copy-start.2 = (bf16[256,768]{1,0:T(8,128)(2,1)S(1)}, bf16[256,768]{1,0:T(8,128)(2,1)}, u32[]{:S(2)}) copy-start(bf16[256,768]{1,0:T(8,128)(2,1)} %constant.22.clone.terms_ref) | copy-start | bytes 1179652
  6.5 43.4 %all-to-all-start = ((bf16[128,24,128]{2,1,0:T(8,128)(2,1)}), bf16[128,24,128]{2,1,0:T(8,128)(2,1)S(1)}, u32[]{:S(2)}, u32[]{:S(2)}) async-start(bf16[128,24,128]{2,1,0:T(8,128)(2,1)} %pack_product.1), calls=%async_computation | async-start | bytes 1572864 | tf_op jit(solution)/shard_map/all_to_all | solution.py:224
  26.5 37.0 %collective-permute-start = (bf16[3,2048,2]{1,2,0:T(2,128)(2,1)S(1)}, bf16[3,2048,2]{1,2,0:T(2,128)(2,1)S(1)}, u32[]{:S(2)}, u32[]{:S(2)}) collective-permute-start(bf16[3,2048,2]{1,2,0:T(2,128)(2,1)S(1)} %slice.45), channel_id=1, source_target_pairs={{0,4},{4,8},{8,12},{12,16},{16,20},{20,24},{24,28},{28,32},{32,36}... | collective-permute-start | bytes 73736 | tf_op jit(solution)/shard_map/ppermute | solution.py:229
  56.2 27.2 %all-to-all-start.1 = ((bf16[128,16,128]{2,1,0:T(8,128)(2,1)}), bf16[128,16,128]{2,1,0:T(8,128)(2,1)}, u32[]{:S(2)}, u32[]{:S(2)}) async-start(bf16[128,16,128]{2,1,0:T(8,128)(2,1)} %bitcast.2), calls=%async_computation.1 | async-start | bytes 1048576 | tf_op jit(solution)/shard_map/all_to_all | solution.py:231
  70.2 0.7 copy-start.5
  70.2 13.2 %copy-start.6 = (f32[2048]{0:T(1024)S(1)}, f32[2048]{0:T(1024)}, u32[]{:S(2)}) copy-start(f32[2048]{0:T(1024)} %param.10) | copy-start | bytes 24580

commit v3 on v2

--- a/solution.py
+++ b/solution.py
@@ -9,7 +9,6 @@
 bf16 = jnp.bfloat16
 f32 = jnp.float32
 LANES = 128
-SLOT = 24
 
 
 def lane_iota(shape):
@@ -24,18 +23,15 @@
 
 
 def pack_product(streams, short_weight, filters, owned):
-    chan = streams.shape[1]
+    taps, _, chan = short_weight.shape
     owners = chan // owned
-    chunk = 256
-    taps = short_weight.shape[0]
-
-    def kernel(key_ref, value_ref, weight_ref, filt_ref, out_ref, ends_ref):
+    chunk = 1024
+    per = chunk // owned
+    terms = 2 * taps
+
+    def kernel(key_ref, value_ref, weight_ref, filt_ref, out_ref):
         src = row_iota((LANES, LANES))
-        dst = lane_iota((LANES, LANES))
-        shifts = jnp.concatenate(
-            [jnp.where(dst == src + j, 1.0, 0.0) for j in range(1, taps)], axis=1
-        ).astype(bf16)
-        place = dst // owned
+        place = lane_iota((LANES, LANES)) // owned
         pick = []
         for stream in range(2):
             hit = jnp.zeros((LANES, LANES), f32)
@@ -43,61 +39,52 @@
                 hit = jnp.where((place == 4 * stream + n) & (src == pos), 1.0, hit)
             pick.append(hit)
         pick = jnp.concatenate(pick, axis=0).astype(bf16)
+        weight = weight_ref[...].reshape(3 * taps, chunk)
+        high = weight.astype(bf16).astype(f32)
+        middle = (weight - high).astype(bf16).astype(f32)
+        parts = [high, middle, weight - high - middle, jnp.zeros((32 - 9 * taps, chunk), f32)]
+        parts = jnp.transpose(jnp.concatenate(parts, axis=0)).astype(bf16)
+        row = row_iota((32, terms * LANES))
+        block = lane_iota((32, terms * LANES)) // LANES
+        wanted = 3 * (block % taps) + block // taps + 1
+        choose = jnp.where((row % (3 * taps) == wanted) & (row < 9 * taps), 1.0, 0.0).astype(bf16)
+        along = jnp.dot(parts, choose, preferred_element_type=f32)
         shape = (chunk, LANES)
-        inner = lane_iota(shape) >= taps - 1
+        convs = []
+        for stream, raw_ref in enumerate((key_ref, value_ref)):
+            raw = raw_ref[0].astype(f32)
+            total = along[:, stream * taps * LANES : (stream * taps + 1) * LANES] * raw
+            for j in range(1, taps):
+                at = (stream * taps + j) * LANES
+                total = total + along[:, at : at + LANES] * pltpu.roll(raw, j, 1)
+            convs.append(total)
+        product = jnp.where(lane_iota(shape) >= taps - 1, convs[0] * convs[1], 0.0).astype(bf16)
+        out_ref[:, 0 : owned // 2] = product.reshape(per, owned // 2, 2, LANES)
         same = lane_iota(shape) % owned == row_iota(shape) % owned
-        ends = jnp.zeros((owners, LANES), f32)
-        for first in range(0, chan, chunk):
-            rows = slice(first, first + chunk)
-            columns = jnp.transpose(weight_ref[:, rows])
-            key = key_ref[0, rows, :]
-            value = value_ref[0, rows, :]
-            convs = []
-            for stream, raw in ((1, key), (2, value)):
-                moved = jnp.dot(raw, shifts, preferred_element_type=f32)
-                total = columns[:, stream : stream + 1] * raw.astype(f32)
-                for j in range(1, taps):
-                    total = total + columns[:, 3 * j + stream : 3 * j + stream + 1] * (
-                        moved[:, (j - 1) * LANES : j * LANES]
-                    )
-                convs.append(total)
-            product = jnp.where(inner, convs[0] * convs[1], 0.0).astype(bf16)
-            out_ref[first // owned : (first + chunk) // owned, 0:owned, :] = product.reshape(
-                chunk // owned, owned, LANES
-            )
-            spread = jnp.dot(jnp.concatenate([key, value], axis=1), pick, preferred_element_type=f32)
-            spread = jnp.where(same, spread, 0.0).astype(bf16)
-            group_shape = (owners, chunk)
-            member = row_iota(group_shape) == (lane_iota(group_shape) + first) // owned
-            ends = ends + jnp.dot(
-                jnp.where(member, 1.0, 0.0).astype(bf16), spread, preferred_element_type=f32
-            )
-        ends_ref[...] = ends
-        sub = row_iota((8, LANES))
-        for owner in range(owners):
-            row = jnp.where(
-                sub == 0,
-                jnp.broadcast_to(filt_ref[owner : owner + 1, :], (8, LANES)),
-                jnp.broadcast_to(ends_ref[owner : owner + 1, :], (8, LANES)),
-            )
-            out_ref[owner, owned : owned + 8, :] = jnp.where(sub < 2, row, 0.0).astype(bf16)
-
-    weights = jnp.pad(short_weight.reshape(3 * taps, chan), ((0, 16 - 3 * taps), (0, 0)))
+        spread = jnp.dot(
+            jnp.concatenate([key_ref[0], value_ref[0]], axis=1), pick, preferred_element_type=f32
+        )
+        spread = jnp.where(same, spread, 0.0).astype(bf16)
+        member = row_iota((per, chunk)) == lane_iota((per, chunk)) // owned
+        ends = jnp.dot(jnp.where(member, 1.0, 0.0).astype(bf16), spread, preferred_element_type=f32)
+        first = row_iota((per, 2, LANES)) == 0
+        rest = jnp.where(first, filt_ref[...][:, None, :], ends[:, None, :])
+        out_ref[:, owned // 2] = rest.astype(bf16)
+
     return pl.pallas_call(
         kernel,
-        grid=(1,),
-        out_shape=jax.ShapeDtypeStruct((owners, SLOT, LANES), bf16),
+        grid=(chan // chunk,),
+        out_shape=jax.ShapeDtypeStruct((owners, owned // 2 + 1, 2, LANES), bf16),
         in_specs=[
-            pl.BlockSpec((1, chan, LANES), lambda i: (1, 0, 0)),
-            pl.BlockSpec((1, chan, LANES), lambda i: (2, 0, 0)),
-            pl.BlockSpec((16, chan), lambda i: (0, 0)),
-            pl.BlockSpec((owners, LANES), lambda i: (0, 0)),
+            pl.BlockSpec((1, chunk, LANES), lambda i: (1, i, 0)),
+            pl.BlockSpec((1, chunk, LANES), lambda i: (2, i, 0)),
+            pl.BlockSpec((taps, 3, chunk), lambda i: (0, 0, i)),
+            pl.BlockSpec((per, LANES), lambda i: (i, 0)),
         ],
-        out_specs=pl.BlockSpec((owners, SLOT, LANES), lambda i: (0, 0, 0)),
-        scratch_shapes=[pltpu.VMEM((owners, LANES), f32)],
+        out_specs=pl.BlockSpec((per, owned // 2 + 1, 2, LANES), lambda i: (i, 0, 0, 0)),
         compiler_params=pltpu.CompilerParams(vmem_limit_bytes=32 << 20),
         name="pack_product",
-    )(streams, streams, weights, filters)
+    )(*(pltpu.with_memory_space_constraint(x, pltpu.HBM) for x in (streams, streams, short_weight, filters)))
 
 
 def end_terms(owned):
@@ -122,7 +109,7 @@
 
     def kernel(recv_ref, weight_ref, terms_ref, out_ref, toep_ref, cols_ref, acc_ref, ends_ref, first_ref):
         for k in range(blocks):
-            ends_ref[k : k + 1, :] = recv_ref[k // 2, k % 2, owned : owned + 8, :].astype(f32)[1:2]
+            ends_ref[k : k + 1, :] = recv_ref[k // 2, k % 2, owned // 2].astype(f32)[1:2]
         ends = ends_ref[...]
         before = jnp.where(row_iota(ends.shape) == 0, 0.0, pltpu.roll(ends, 1, 0))
         both = jnp.concatenate([ends, before], axis=1).astype(bf16)
@@ -149,7 +136,7 @@
                 spread = jnp.dot(member, first_ref[...], preferred_element_type=f32)
                 spread = jnp.where(same, spread, 0.0).astype(bf16)
                 patch = jnp.dot(spread, to_lane, preferred_element_type=f32)
-                part = recv_ref[begin // owned : (begin + chunk) // owned, parity, 0:owned, :]
+                part = recv_ref[begin // owned : (begin + chunk) // owned, parity, 0 : owned // 2]
                 part = (part.reshape(chunk, LANES).astype(f32) + patch).astype(bf16)
                 for lag in range(span):
                     top = begin + lag * owned
@@ -162,7 +149,7 @@
 
         def build(first, count, before):
             for k in range(first, first + count):
-                taps = recv_ref[k // 2, k % 2, owned : owned + 8, :].astype(f32)[0:1]
+                taps = recv_ref[k // 2, k % 2, owned // 2].astype(f32)[0:1]
                 turned = pltpu.roll(jnp.broadcast_to(taps, (LANES, LANES)), 0, 1, stride=1, stride_axis=0)
                 toep_ref[k + 1] = jnp.where(upper, turned, before).astype(bf16)
                 before = turned
@@ -198,7 +185,7 @@
         ],
         compiler_params=pltpu.CompilerParams(vmem_limit_bytes=32 << 20),
         name="long_conv",
-    )(recv.reshape(half, 2, recv.shape[1], LANES), own_weight, end_terms(owned))
+    )(recv.reshape((half, 2) + recv.shape[1:]), own_weight, end_terms(owned))
     return out.reshape(blocks, owned, LANES)
 
 
@@ -211,6 +198,53 @@
         start = taps - 1 - offset
         conv = conv + short_weight[offset][:, :, None] * padded[:, :, start : start + length]
     return lax.optimization_barrier((conv[0].astype(bf16), (conv[1] * conv[2]).astype(bf16)))
+
+
+def in_vmem(*arrays):
+    return tuple(pltpu.with_memory_space_constraint(x, pltpu.VMEM) for x in arrays)
+
+
+def gate(back, query, direct, gain):
+    chan, length = query.shape
+    chunk = chan // 4
+
+    def kernel(back_ref, query_ref, direct_ref, gain_ref, out_ref, sum_ref):
+        total = jnp.zeros((8, length), f32)
+        for first in range(0, chan, chunk):
+            rows = slice(first, first + chunk)
+            mixed = back_ref[rows, :].astype(f32) + direct_ref[rows, :]
+            gated = (query_ref[rows, :].astype(f32) * mixed).astype(bf16).astype(f32)
+            out_ref[rows, :] = gated * gain_ref[rows, :]
+            total = total + jnp.sum((gated * gated).reshape(chunk // 8, 8, length), axis=0)
+        sum_ref[...] = jnp.sum(total, axis=0, keepdims=True)
+
+    whole = pl.BlockSpec(memory_space=pltpu.VMEM)
+    return pl.pallas_call(
+        kernel,
+        out_shape=(pltpu.VMEM((chan, length), f32), pltpu.VMEM((1, length), f32)),
+        in_specs=[whole] * 4,
+        out_specs=(whole, whole),
+        compiler_params=pltpu.CompilerParams(vmem_limit_bytes=16 << 20),
+        name="gate",
+    )(*in_vmem(back, query, direct, gain))
+
+
+def finish(gated, squares, count):
+    chan, length = gated.shape
+
+    def kernel(gated_ref, squares_ref, out_ref):
+        rms = jnp.sqrt(jnp.sum(squares_ref[...], axis=0) / count + 1e-05)
+        out_ref[...] = (gated_ref[...] * (1.0 / rms)).astype(bf16)
+
+    whole = pl.BlockSpec(memory_space=pltpu.VMEM)
+    return pl.pallas_call(
+        kernel,
+        out_shape=jax.ShapeDtypeStruct((chan, length), bf16),
+        in_specs=[whole, whole],
+        out_specs=whole,
+        compiler_params=pltpu.CompilerParams(vmem_limit_bytes=16 << 20),
+        name="finish",
+    )(*in_vmem(gated), squares)
 
 
 def shards(streams, short_weight, filters, skip_gain, norm_gain):
@@ -233,14 +267,12 @@
         (streams, tail, short_weight, skip_gain, norm_gain, mixed)
     )
     query, product = local_streams(streams, tail, short_weight)
+    gain = jnp.broadcast_to(norm_gain[:, None], (local_chan, length))
+    gain, product = lax.optimization_barrier((gain, product))
     direct = skip_gain[:, None] * product.astype(f32)
-    gain = jnp.broadcast_to(norm_gain[:, None], (local_chan, length))
     direct, gain, query, back = lax.optimization_barrier((direct, gain, query, back))
-    gated = (query.astype(f32) * (back.astype(f32) + direct)).astype(bf16)
-    gated_wide = lax.optimization_barrier(gated).astype(f32)
-    squares = jnp.sum(lax.all_gather(jnp.sum(gated_wide * gated_wide, axis=0), "tp"), axis=0)
-    rms = jnp.sqrt(squares / (local_chan * n_width) + 1e-05)
-    return (gated_wide * gain / rms[None, :]).astype(bf16)
+    gated, squares = gate(back, query, direct, gain)
+    return finish(gated, lax.all_gather(squares, "tp"), local_chan * n_width)
 
 
 def solution(mesh):

time: 96.4 us -> 88.6 us (0.919)
  waiting for transfers between devices: 33.2 us -> 26.9 us
  Pallas kernels: 9.64 us -> 12.3 us
  local copies, waits for them, and re-layouts: 7.68 us -> 5.29 us
  other arithmetic: 8.71 us -> 7.65 us
    all_to_all x1, waiting for transfers between devices: 21.1 us -> 16.9 us  [shards(): recv = lax.all_to_all(send, 'ctx', 0, 0)]
    unnamed x14 -> x12, local copies, waits for them, and re-layouts: 2.76 us -> 0.53 us
    convert_element_type x2 -> x0, other arithmetic: 2.16 us -> none  [the longest x1 1.22 us: shards(): gated = (query.astype(f32) * (back.astype(f32) + direct)).astype(bf16)]
    all_to_all x1, waiting for transfers between devices: 12.2 us -> 10 us  [shards(): back = lax.all_to_all(mixed, 'ctx', 0, 0).reshape(local_chan, length)]
    pallas_call x1 -> x3, Pallas kernels: 3.28 us -> 5.37 us  [the longest x1 4.2 us: pack_product(): pl.pallas_call(kernel, grid=(chan // chunk,), out_shape=jax.ShapeDtypeStr...]
    convert_element_type x1, other arithmetic: 1.13 us -> 2.54 us  [local_streams(): padded = jnp.concatenate([tail, streams], axis=2).astype(f32)]
  transfers between devices with their start and end apart: 3 -> 3, of which waited for: 2 -> 2; matrix products, arithmetic and copies ran while one was open for 10% -> 14% of each run, Pallas kernels for 7% -> 8%
where the time goes in v3:
time: 88.6 us; the launch traced here: 88.2 us
  waiting for transfers between devices  26.9 us (30%)
  starting transfers between devices  26.2 us (30%)
  Pallas kernels  12.3 us (14%)
  blocking collectives  9.68 us (11%)
  other arithmetic  7.65 us (9%)
  local copies, waits for them, and re-layouts  5.29 us (6%)
    all_to_all x1, starting transfers between devices, shards(): recv = lax.all_to_all(send, 'ctx', 0, 0)  17.5 us
    all_to_all x1, waiting for transfers between devices, shards(): recv = lax.all_to_all(send, 'ctx', 0, 0)  16.9 us
    all_to_all x1, waiting for transfers between devices, shards(): back = lax.all_to_all(mixed, 'ctx', 0, 0).reshape(local_chan, length)  10 us
    all_gather x1, blocking collectives, shards(): return finish(gated, lax.all_gather(squares, 'tp'), local_chan * n_width)  9.68 us
    pallas_call x1, Pallas kernels, long_conv_blocks(): pl.pallas_call(kernel, out_shape=jax.ShapeDtypeStruct((half, 2, owned, LA...  6.96 us
    all_to_all x1, starting transfers between devices, shards(): back = lax.all_to_all(mixed, 'ctx', 0, 0).reshape(local_chan, length)  6.67 us
    add x1, other arithmetic, local_streams(): conv + short_weight[offset][:, :, None] * padded[:, :, start:start + length]  4.67 us
    pallas_call x1, Pallas kernels, pack_product(): pl.pallas_call(kernel, grid=(chan // chunk,), out_shape=jax.ShapeDtypeStr...  4.2 us
  transfers between devices with their start and end apart: 3, of which 2 were waited for; matrix products, arithmetic and copies ran while one was open for 14% of the time, Pallas kernels for 8%

profile of v3, /device:TPU:8, one launch (start us, length us, event | category | flops | bytes accessed | tf_op | source)
XLA Modules:
  0.0 88.2 jit_solution(6634091480830006709)
XLA Ops:
  0.0 0.0 copy-start.1
  0.0 4.2 %pack_product.1 = bf16[128,9,2,128]{3,2,1,0:T(2,128)(2,1)} custom-call(bf16[3,2048,128]{2,1,0:T(8,128)(2,1)} %value_ref.1, bf16[3,2048,128]{2,1,0:T(8,128)(2,1)} %value_ref.1, f32[3,3,2048]{2,1,0:T(4,128)} %weight_ref.1, f32[128,128]{1,0:T(8,128)} %filt_ref.1), custom_call_target="tpu_custom_call" | custom-call | tf_op jit(solution)/shard_map/pack_product/pallas_call | solution.py:74
  4.2 0.0 copy-start.3
  4.2 17.5 %all-to-all-start = ((bf16[128,9,2,128]{3,2,1,0:T(2,128)(2,1)}), bf16[128,9,2,128]{3,2,1,0:T(2,128)(2,1)S(1)}, u32[]{:S(2)}, u32[]{:S(2)}) async-start(bf16[128,9,2,128]{3,2,1,0:T(2,128)(2,1)} %pack_product.1), calls=%async_computation | async-start | bytes 1179648 | tf_op jit(solution)/shard_map/all_to_all | solution.py:258
  21.7 0.0 copy-done.1
  21.7 1.6 %copy.9 = bf16[3,2048,128]{1,2,0:T(8,128)(2,1)} copy(bf16[3,2048,128]{2,1,0:T(8,128)(2,1)S(1)} %copy-done.1) | data formatting | bytes 3145728 | tf_op jit(solution)/shard_map/optimization_barrier | solution.py:259
  23.3 0.9 %slice.45 = bf16[3,2048,2]{1,2,0:T(2,128)(2,1)S(1)} slice(bf16[3,2048,128]{1,2,0:T(8,128)(2,1)} %copy.9), slice={[0:3], [0:2048], [126:128]} | slice | bytes 49152 | tf_op jit(solution)/shard_map/slice | solution.py:263
  24.3 2.1 %collective-permute-start = (bf16[3,2048,2]{1,2,0:T(2,128)(2,1)S(1)}, bf16[3,2048,2]{1,2,0:T(2,128)(2,1)S(1)}, u32[]{:S(2)}, u32[]{:S(2)}) collective-permute-start(bf16[3,2048,2]{1,2,0:T(2,128)(2,1)S(1)} %slice.45), channel_id=1, source_target_pairs={{0,4},{4,8},{8,12},{12,16},{16,20},{20,24},{24,28},{28,32},{32,36}... | collective-permute-start | bytes 73736 | tf_op jit(solution)/shard_map/ppermute | solution.py:263
  26.3 0.0 copy-done.3
  26.4 0.1 dynamic-slice_bitcast_fusion
  26.5 0.1 tile.12
  26.5 16.9 %all-to-all-done = bf16[128,9,2,128]{3,2,1,0:T(2,128)(2,1)S(1)} async-done(((bf16[128,9,2,128]{3,2,1,0:T(2,128)(2,1)}), bf16[128,9,2,128]{3,2,1,0:T(2,128)(2,1)S(1)}, u32[]{:S(2)}, u32[]{:S(2)}) %all-to-all-start) | async-done | bytes 589856 | tf_op jit(solution)/shard_map/all_to_all | solution.py:258
  43.4 0.0 copy-done
  43.4 7.0 %long_conv.1 = bf16[64,2,16,128]{3,2,1,0:T(8,128)(2,1)} custom-call(bf16[64,2,9,2,128]{4,3,2,1,0:T(2,128)(2,1)S(1)} %bitcast.16, f32[8,128]{1,0:T(8,128)S(1)} %pad.4.weight_ref, bf16[256,768]{1,0:T(8,128)(2,1)S(1)} %copy-done), custom_call_target="tpu_custom_call" | custom-call | tf_op jit(solution)/shard_map/long_conv/pallas_call | solution.py:174
  50.4 6.7 %all-to-all-start.1 = ((bf16[128,16,128]{2,1,0:T(8,128)(2,1)}), bf16[128,16,128]{2,1,0:T(8,128)(2,1)S(1)}, u32[]{:S(2)}, u32[]{:S(2)}) async-start(bf16[128,16,128]{2,1,0:T(8,128)(2,1)} %bitcast.2), calls=%async_computation.1 | async-start | bytes 1048576 | tf_op jit(solution)/shard_map/all_to_all | solution.py:265
  57.0 0.0 collective-permute-done
  57.0 1.6 %copy.11 = bf16[3,2048,2]{2,1,0:T(8,128)(2,1)} copy(bf16[3,2048,2]{1,2,0:T(2,128)(2,1)S(1)} %collective-permute-done) | data formatting | bytes 49152 | tf_op jit(solution)/shard_map/optimization_barrier | solution.py:266
  58.7 0.0 copy-done.2
  58.7 2.5 %maximum_convert_fusion = f32[3,2048,130]{2,1,0:T(8,128)S(1)} fusion(bf16[3,2048,128]{2,1,0:T(8,128)(2,1)S(1)} %copy-done.2, bf16[3,2048,2]{2,1,0:T(8,128)(2,1)} %copy.11), kind=kLoop, calls=%fused_computation.5 | loop fusion | flops 3194880 | bytes 4792320 | tf_op jit(solution)/shard_map/convert_element_type | solution.py:195
  61.2 4.7 %fusion = f32[3,2048,128]{2,1,0:T(8,128)S(1)} fusion(f32[3,2048,130]{2,1,0:T(8,128)S(1)} %maximum_convert_fusion, f32[3,2048]{1,0:T(4,128)S(1)} %get-tuple-element.40, f32[3,2048]{1,0:T(4,128)S(1)} %get-tuple-element.41, f32[3,2048]{1,0:T(4,128)S(1)} %get-tuple-element.39), kind=kLoop, calls=%fused_computation.1 | loop fusion | flops 3932160 | bytes 12656640 | tf_op jit(solution)/shard_map/add | solution.py:199
  65.9 0.0 copy-start.4
  65.9 0.0 copy-start.5
  66.0 0.1 fusion.3.query_ref
  66.0 0.1 fusion.4
  66.1 0.5 copy-done.4
  66.6 0.3 broadcast_in_dim.2.gain_ref
  67.0 0.0 copy-done.5
  67.0 0.3 convert_multiply_fusion.direct_ref
  67.3 10.0 %all-to-all-done.1 = bf16[128,16,128]{2,1,0:T(8,128)(2,1)S(1)} async-done(((bf16[128,16,128]{2,1,0:T(8,128)(2,1)}), bf16[128,16,128]{2,1,0:T(8,128)(2,1)S(1)}, u32[]{:S(2)}, u32[]{:S(2)}) %all-to-all-start.1) | async-done | bytes 524320 | tf_op jit(solution)/shard_map/all_to_all | solution.py:265
  77.4 0.3 gate.1
  77.7 9.7 %all-gather.1.squares_ref = f32[4,1,128]{2,1,0:T(1,128)S(1)} all-gather(f32[1,1,128]{2,1,0:T(1,128)S(1)} %bitcast.18), channel_id=2, replica_groups=mesh['ctx'=128,'tp'=4] {'tp'}, dimensions={0}, use_global_device_ids=true | all-gather | bytes 2560 | tf_op jit(solution)/shard_map/all_gather | solution.py:275
  87.3 0.9 finish.1
  (7 shorter events, 0.1 us)
Async XLA Ops:
  0.0 21.7 %copy-start.1 = (bf16[3,2048,128]{2,1,0:T(8,128)(2,1)S(1)}, bf16[3,2048,128]{2,1,0:T(8,128)(2,1)}, u32[]{:S(2)}) copy-start(bf16[3,2048,128]{2,1,0:T(8,128)(2,1)} %value_ref.1) | copy-start | bytes 4718596
  4.2 22.1 %copy-start.3 = (f32[3,3,2048]{2,1,0:T(4,128)S(1)}, f32[3,3,2048]{2,1,0:T(4,128)}, u32[]{:S(2)}) copy-start(f32[3,3,2048]{2,1,0:T(4,128)} %weight_ref.1) | copy-start | bytes 221188
  4.2 39.2 %copy-start = (bf16[256,768]{1,0:T(8,128)(2,1)S(1)}, bf16[256,768]{1,0:T(8,128)(2,1)}, u32[]{:S(2)}) copy-start(bf16[256,768]{1,0:T(8,128)(2,1)} %constant.16.clone.terms_ref) | copy-start | bytes 1179652
  4.2 39.2 %all-to-all-start = ((bf16[128,9,2,128]{3,2,1,0:T(2,128)(2,1)}), bf16[128,9,2,128]{3,2,1,0:T(2,128)(2,1)S(1)}, u32[]{:S(2)}, u32[]{:S(2)}) async-start(bf16[128,9,2,128]{3,2,1,0:T(2,128)(2,1)} %pack_product.1), calls=%async_computation | async-start | bytes 1179648 | tf_op jit(solution)/shard_map/all_to_all | solution.py:258
  24.3 32.8 %collective-permute-start = (bf16[3,2048,2]{1,2,0:T(2,128)(2,1)S(1)}, bf16[3,2048,2]{1,2,0:T(2,128)(2,1)S(1)}, u32[]{:S(2)}, u32[]{:S(2)}) collective-permute-start(bf16[3,2048,2]{1,2,0:T(2,128)(2,1)S(1)} %slice.45), channel_id=1, source_target_pairs={{0,4},{4,8},{8,12},{12,16},{16,20},{20,24},{24,28},{28,32},{32,36}... | collective-permute-start | bytes 73736 | tf_op jit(solution)/shard_map/ppermute | solution.py:263
  50.4 8.3 %copy-start.2 = (bf16[3,2048,128]{2,1,0:T(8,128)(2,1)S(1)}, bf16[3,2048,128]{2,1,0:T(8,128)(2,1)}, u32[]{:S(2)}) copy-start(bf16[3,2048,128]{2,1,0:T(8,128)(2,1)} %value_ref.1) | copy-start | bytes 4718596
  50.4 27.0 %all-to-all-start.1 = ((bf16[128,16,128]{2,1,0:T(8,128)(2,1)}), bf16[128,16,128]{2,1,0:T(8,128)(2,1)S(1)}, u32[]{:S(2)}, u32[]{:S(2)}) async-start(bf16[128,16,128]{2,1,0:T(8,128)(2,1)} %bitcast.2), calls=%async_computation.1 | async-start | bytes 1048576 | tf_op jit(solution)/shard_map/all_to_all | solution.py:265
  65.9 0.7 copy-start.4
  65.9 1.0 %copy-start.5 = (f32[2048]{0:T(1024)S(1)}, f32[2048]{0:T(1024)}, u32[]{:S(2)}) copy-start(f32[2048]{0:T(1024)} %param.9) | copy-start | bytes 24580

commit v4 on v3

--- a/solution.py
+++ b/solution.py
@@ -49,27 +49,30 @@
         wanted = 3 * (block % taps) + block // taps + 1
         choose = jnp.where((row % (3 * taps) == wanted) & (row < 9 * taps), 1.0, 0.0).astype(bf16)
         along = jnp.dot(parts, choose, preferred_element_type=f32)
-        shape = (chunk, LANES)
-        convs = []
-        for stream, raw_ref in enumerate((key_ref, value_ref)):
-            raw = raw_ref[0].astype(f32)
-            total = along[:, stream * taps * LANES : (stream * taps + 1) * LANES] * raw
-            for j in range(1, taps):
-                at = (stream * taps + j) * LANES
-                total = total + along[:, at : at + LANES] * pltpu.roll(raw, j, 1)
-            convs.append(total)
-        product = jnp.where(lane_iota(shape) >= taps - 1, convs[0] * convs[1], 0.0).astype(bf16)
-        out_ref[:, 0 : owned // 2] = product.reshape(per, owned // 2, 2, LANES)
+        part = chunk // 2
+        shape = (part, LANES)
+        inner = lane_iota(shape) >= taps - 1
         same = lane_iota(shape) % owned == row_iota(shape) % owned
-        spread = jnp.dot(
-            jnp.concatenate([key_ref[0], value_ref[0]], axis=1), pick, preferred_element_type=f32
-        )
-        spread = jnp.where(same, spread, 0.0).astype(bf16)
-        member = row_iota((per, chunk)) == lane_iota((per, chunk)) // owned
-        ends = jnp.dot(jnp.where(member, 1.0, 0.0).astype(bf16), spread, preferred_element_type=f32)
-        first = row_iota((per, 2, LANES)) == 0
-        rest = jnp.where(first, filt_ref[...][:, None, :], ends[:, None, :])
-        out_ref[:, owned // 2] = rest.astype(bf16)
+        for begin in range(0, chunk, part):
+            rows = slice(begin, begin + part)
+            own = slice(begin // owned, (begin + part) // owned)
+            along = jnp.dot(parts[rows], choose, preferred_element_type=f32)
+            convs = []
+            for stream, raw_ref in enumerate((key_ref, value_ref)):
+                raw = raw_ref[0, rows]
+                total = along[:, stream * taps * LANES : (stream * taps + 1) * LANES] * raw.astype(f32)
+                for j in range(1, taps):
+                    at = (stream * taps + j) * LANES
+                    total = total + along[:, at : at + LANES] * pltpu.roll(raw, j, 1).astype(f32)
+                convs.append(total)
+            product = jnp.where(inner, convs[0] * convs[1], 0.0).astype(bf16)
+            out_ref[own, 0 : owned // 2] = product.reshape(part // owned, owned // 2, 2, LANES)
+            both = jnp.concatenate([key_ref[0, rows], value_ref[0, rows]], axis=1)
+            spread = jnp.where(same, jnp.dot(both, pick, preferred_element_type=f32), 0.0)
+            ends = jnp.sum(spread.reshape(part // owned, owned, LANES), axis=1)
+            first = row_iota((part // owned, 2, LANES)) == 0
+            rest = jnp.where(first, filt_ref[own][:, None, :], ends[:, None, :])
+            out_ref[own, owned // 2] = rest.astype(bf16)
 
     return pl.pallas_call(
         kernel,
@@ -121,9 +124,9 @@
                 at = 3 * stream + n
                 total = total + weight_ref[at : at + 1, :] * terms[:, at * LANES : (at + 1) * LANES]
             convs.append(total)
-        first_ref[...] = (convs[0] * convs[1]).astype(bf16)
-        shape = (chunk, LANES)
-        same = lane_iota(shape) % owned == row_iota(shape) % owned
+        first_ref[...] = (convs[0] * convs[1]).astype(bf16).astype(f32)
+        shape = (owned, LANES)
+        same = lane_iota(shape) % owned == row_iota(shape)
         src = row_iota((LANES, LANES))
         dst = lane_iota((LANES, LANES))
         to_lane = jnp.where((src // owned == dst) & (dst < 2), 1.0, 0.0).astype(bf16)
@@ -131,10 +134,12 @@
             cols_ref[0 : lag * owned, lag * wide : (lag + 1) * wide] = jnp.zeros((lag * owned, wide), bf16)
         for parity in range(2):
             for begin in range(0, rows, chunk):
-                block = 2 * ((row_iota(shape) + begin) // owned) + parity
-                member = jnp.where(lane_iota(shape) == block, 1.0, 0.0).astype(bf16)
-                spread = jnp.dot(member, first_ref[...], preferred_element_type=f32)
-                spread = jnp.where(same, spread, 0.0).astype(bf16)
+                spread = []
+                for pair in range(begin // owned, (begin + chunk) // owned):
+                    block = 2 * pair + parity
+                    values = jnp.broadcast_to(first_ref[block : block + 1, :], shape)
+                    spread.append(jnp.where(same, values, 0.0))
+                spread = jnp.concatenate(spread, axis=0).astype(bf16)
                 patch = jnp.dot(spread, to_lane, preferred_element_type=f32)
                 part = recv_ref[begin // owned : (begin + chunk) // owned, parity, 0 : owned // 2]
                 part = (part.reshape(chunk, LANES).astype(f32) + patch).astype(bf16)
@@ -181,7 +186,7 @@
             pltpu.VMEM((rows, span * wide), bf16),
             pltpu.VMEM((rows, wide), f32),
             pltpu.VMEM((blocks, LANES), f32),
-            pltpu.VMEM((blocks, LANES), bf16),
+            pltpu.VMEM((blocks, LANES), f32),
         ],
         compiler_params=pltpu.CompilerParams(vmem_limit_bytes=32 << 20),
         name="long_conv",
@@ -232,16 +237,27 @@
 def finish(gated, squares, count):
     chan, length = gated.shape
 
-    def kernel(gated_ref, squares_ref, out_ref):
-        rms = jnp.sqrt(jnp.sum(squares_ref[...], axis=0) / count + 1e-05)
-        out_ref[...] = (gated_ref[...] * (1.0 / rms)).astype(bf16)
+    parts = 4
+    chunk = chan // parts
+
+    def kernel(gated_ref, squares_ref, out_ref, done_ref, sems):
+        scale = 1.0 / jnp.sqrt(jnp.sum(squares_ref[...], axis=0) / count + 1e-05)
+        copies = []
+        for part in range(parts):
+            rows = pl.ds(part * chunk, chunk)
+            done_ref[rows, :] = (gated_ref[rows, :] * scale).astype(bf16)
+            copies.append(pltpu.make_async_copy(done_ref.at[rows], out_ref.at[rows], sems.at[part]))
+            copies[part].start()
+        for copy in copies:
+            copy.wait()
 
     whole = pl.BlockSpec(memory_space=pltpu.VMEM)
     return pl.pallas_call(
         kernel,
         out_shape=jax.ShapeDtypeStruct((chan, length), bf16),
         in_specs=[whole, whole],
-        out_specs=whole,
+        out_specs=pl.BlockSpec(memory_space=pltpu.HBM),
+        scratch_shapes=[pltpu.VMEM((chan, length), bf16), pltpu.SemaphoreType.DMA((parts,))],
         compiler_params=pltpu.CompilerParams(vmem_limit_bytes=16 << 20),
         name="finish",
     )(*in_vmem(gated), squares)

time: 88.6 us -> 88 us (level)
  no operation moved by 1% of the time
where the time goes in v4:
time: 88 us; the launch traced here: 87.6 us
  waiting for transfers between devices  26.9 us (31%)
  starting transfers between devices  26.2 us (30%)
  Pallas kernels  11.6 us (13%)
  blocking collectives  9.67 us (11%)
  other arithmetic  7.65 us (9%)
  local copies, waits for them, and re-layouts  5.29 us (6%)
    all_to_all x1, starting transfers between devices, shards(): recv = lax.all_to_all(send, 'ctx', 0, 0)  17.5 us
    all_to_all x1, waiting for transfers between devices, shards(): recv = lax.all_to_all(send, 'ctx', 0, 0)  16.9 us
    all_to_all x1, waiting for transfers between devices, shards(): back = lax.all_to_all(mixed, 'ctx', 0, 0).reshape(local_chan, length)  10 us
    all_gather x1, blocking collectives, shards(): return finish(gated, lax.all_gather(squares, 'tp'), local_chan * n_width)  9.67 us
    all_to_all x1, starting transfers between devices, shards(): back = lax.all_to_all(mixed, 'ctx', 0, 0).reshape(local_chan, length)  6.67 us
    pallas_call x1, Pallas kernels, long_conv_blocks(): pl.pallas_call(kernel, out_shape=jax.ShapeDtypeStruct((half, 2, owned, LA...  6.63 us
    add x1, other arithmetic, local_streams(): conv + short_weight[offset][:, :, None] * padded[:, :, start:start + length]  4.67 us
    pallas_call x1, Pallas kernels, pack_product(): pl.pallas_call(kernel, grid=(chan // chunk,), out_shape=jax.ShapeDtypeStr...  3.81 us
  transfers between devices with their start and end apart: 3, of which 2 were waited for; matrix products, arithmetic and copies ran while one was open for 14% of the time, Pallas kernels for 8%

profile of v4, /device:TPU:8, one launch (start us, length us, event | category | flops | bytes accessed | tf_op | source)
XLA Modules:
  0.0 87.6 jit_solution(610093095881278725)
XLA Ops:
  0.0 0.0 copy-start.1
  0.0 3.8 %pack_product.1 = bf16[128,9,2,128]{3,2,1,0:T(2,128)(2,1)} custom-call(bf16[3,2048,128]{2,1,0:T(8,128)(2,1)} %value_ref.1, bf16[3,2048,128]{2,1,0:T(8,128)(2,1)} %value_ref.1, f32[3,3,2048]{2,1,0:T(4,128)} %weight_ref.1, f32[128,128]{1,0:T(8,128)} %filt_ref.1), custom_call_target="tpu_custom_call" | custom-call | tf_op jit(solution)/shard_map/pack_product/pallas_call | solution.py:77
  3.8 0.0 copy-start.3
  3.8 17.5 %all-to-all-start = ((bf16[128,9,2,128]{3,2,1,0:T(2,128)(2,1)}), bf16[128,9,2,128]{3,2,1,0:T(2,128)(2,1)S(1)}, u32[]{:S(2)}, u32[]{:S(2)}) async-start(bf16[128,9,2,128]{3,2,1,0:T(2,128)(2,1)} %pack_product.1), calls=%async_computation | async-start | bytes 1179648 | tf_op jit(solution)/shard_map/all_to_all | solution.py:274
  21.3 0.0 copy-done.1
  21.3 1.6 %copy.9 = bf16[3,2048,128]{1,2,0:T(8,128)(2,1)} copy(bf16[3,2048,128]{2,1,0:T(8,128)(2,1)S(1)} %copy-done.1) | data formatting | bytes 3145728 | tf_op jit(solution)/shard_map/optimization_barrier | solution.py:275
  23.0 0.9 %slice.45 = bf16[3,2048,2]{1,2,0:T(2,128)(2,1)S(1)} slice(bf16[3,2048,128]{1,2,0:T(8,128)(2,1)} %copy.9), slice={[0:3], [0:2048], [126:128]} | slice | bytes 49152 | tf_op jit(solution)/shard_map/slice | solution.py:279
  23.9 2.1 %collective-permute-start = (bf16[3,2048,2]{1,2,0:T(2,128)(2,1)S(1)}, bf16[3,2048,2]{1,2,0:T(2,128)(2,1)S(1)}, u32[]{:S(2)}, u32[]{:S(2)}) collective-permute-start(bf16[3,2048,2]{1,2,0:T(2,128)(2,1)S(1)} %slice.45), channel_id=1, source_target_pairs={{0,4},{4,8},{8,12},{12,16},{16,20},{20,24},{24,28},{28,32},{32,36}... | collective-permute-start | bytes 73736 | tf_op jit(solution)/shard_map/ppermute | solution.py:279
  26.0 0.0 copy-done.3
  26.0 0.1 dynamic-slice_bitcast_fusion
  26.1 0.1 tile.12
  26.2 16.9 %all-to-all-done = bf16[128,9,2,128]{3,2,1,0:T(2,128)(2,1)S(1)} async-done(((bf16[128,9,2,128]{3,2,1,0:T(2,128)(2,1)}), bf16[128,9,2,128]{3,2,1,0:T(2,128)(2,1)S(1)}, u32[]{:S(2)}, u32[]{:S(2)}) %all-to-all-start) | async-done | bytes 589856 | tf_op jit(solution)/shard_map/all_to_all | solution.py:274
  43.0 0.0 copy-done
  43.0 6.6 %long_conv.1 = bf16[64,2,16,128]{3,2,1,0:T(8,128)(2,1)} custom-call(bf16[64,2,9,2,128]{4,3,2,1,0:T(2,128)(2,1)S(1)} %bitcast.16, f32[8,128]{1,0:T(8,128)S(1)} %pad.4.weight_ref, bf16[256,768]{1,0:T(8,128)(2,1)S(1)} %copy-done), custom_call_target="tpu_custom_call" | custom-call | tf_op jit(solution)/shard_map/long_conv/pallas_call | solution.py:179
  49.7 6.7 %all-to-all-start.1 = ((bf16[128,16,128]{2,1,0:T(8,128)(2,1)}), bf16[128,16,128]{2,1,0:T(8,128)(2,1)S(1)}, u32[]{:S(2)}, u32[]{:S(2)}) async-start(bf16[128,16,128]{2,1,0:T(8,128)(2,1)} %bitcast.2), calls=%async_computation.1 | async-start | bytes 1048576 | tf_op jit(solution)/shard_map/all_to_all | solution.py:281
  56.3 0.0 collective-permute-done
  56.4 1.6 %copy.11 = bf16[3,2048,2]{2,1,0:T(8,128)(2,1)} copy(bf16[3,2048,2]{1,2,0:T(2,128)(2,1)S(1)} %collective-permute-done) | data formatting | bytes 49152 | tf_op jit(solution)/shard_map/optimization_barrier | solution.py:282
  58.0 0.0 copy-done.2
  58.0 2.5 %maximum_convert_fusion = f32[3,2048,130]{2,1,0:T(8,128)S(1)} fusion(bf16[3,2048,128]{2,1,0:T(8,128)(2,1)S(1)} %copy-done.2, bf16[3,2048,2]{2,1,0:T(8,128)(2,1)} %copy.11), kind=kLoop, calls=%fused_computation.5 | loop fusion | flops 3194880 | bytes 4792320 | tf_op jit(solution)/shard_map/convert_element_type | solution.py:200
  60.5 4.7 %fusion = f32[3,2048,128]{2,1,0:T(8,128)S(1)} fusion(f32[3,2048,130]{2,1,0:T(8,128)S(1)} %maximum_convert_fusion, f32[3,2048]{1,0:T(4,128)S(1)} %get-tuple-element.40, f32[3,2048]{1,0:T(4,128)S(1)} %get-tuple-element.41, f32[3,2048]{1,0:T(4,128)S(1)} %get-tuple-element.39), kind=kLoop, calls=%fused_computation.1 | loop fusion | flops 3932160 | bytes 12656640 | tf_op jit(solution)/shard_map/add | solution.py:204
  65.2 0.0 copy-start.4
  65.2 0.0 copy-start.5
  65.3 0.1 fusion.3.query_ref
  65.3 0.1 fusion.4
  65.4 0.5 copy-done.4
  65.9 0.3 broadcast_in_dim.2.gain_ref
  66.3 0.0 copy-done.5
  66.3 0.3 convert_multiply_fusion.direct_ref
  66.6 10.0 %all-to-all-done.1 = bf16[128,16,128]{2,1,0:T(8,128)(2,1)S(1)} async-done(((bf16[128,16,128]{2,1,0:T(8,128)(2,1)}), bf16[128,16,128]{2,1,0:T(8,128)(2,1)S(1)}, u32[]{:S(2)}, u32[]{:S(2)}) %all-to-all-start.1) | async-done | bytes 524320 | tf_op jit(solution)/shard_map/all_to_all | solution.py:281
  76.7 0.3 gate.1
  77.0 9.7 %all-gather.1.squares_ref = f32[4,1,128]{2,1,0:T(1,128)S(1)} all-gather(f32[1,1,128]{2,1,0:T(1,128)S(1)} %bitcast.18), channel_id=2, replica_groups=mesh['ctx'=128,'tp'=4] {'tp'}, dimensions={0}, use_global_device_ids=true | all-gather | bytes 2560 | tf_op jit(solution)/shard_map/all_gather | solution.py:291
  86.6 0.9 finish.1
  (7 shorter events, 0.1 us)
Async XLA Ops:
  0.0 21.3 %copy-start.1 = (bf16[3,2048,128]{2,1,0:T(8,128)(2,1)S(1)}, bf16[3,2048,128]{2,1,0:T(8,128)(2,1)}, u32[]{:S(2)}) copy-start(bf16[3,2048,128]{2,1,0:T(8,128)(2,1)} %value_ref.1) | copy-start | bytes 4718596
  3.8 22.2 %copy-start.3 = (f32[3,3,2048]{2,1,0:T(4,128)S(1)}, f32[3,3,2048]{2,1,0:T(4,128)}, u32[]{:S(2)}) copy-start(f32[3,3,2048]{2,1,0:T(4,128)} %weight_ref.1) | copy-start | bytes 221188
  3.8 39.2 %copy-start = (bf16[256,768]{1,0:T(8,128)(2,1)S(1)}, bf16[256,768]{1,0:T(8,128)(2,1)}, u32[]{:S(2)}) copy-start(bf16[256,768]{1,0:T(8,128)(2,1)} %constant.16.clone.terms_ref) | copy-start | bytes 1179652
  3.8 39.2 %all-to-all-start = ((bf16[128,9,2,128]{3,2,1,0:T(2,128)(2,1)}), bf16[128,9,2,128]{3,2,1,0:T(2,128)(2,1)S(1)}, u32[]{:S(2)}, u32[]{:S(2)}) async-start(bf16[128,9,2,128]{3,2,1,0:T(2,128)(2,1)} %pack_product.1), calls=%async_computation | async-start | bytes 1179648 | tf_op jit(solution)/shard_map/all_to_all | solution.py:274
  23.9 32.4 %collective-permute-start = (bf16[3,2048,2]{1,2,0:T(2,128)(2,1)S(1)}, bf16[3,2048,2]{1,2,0:T(2,128)(2,1)S(1)}, u32[]{:S(2)}, u32[]{:S(2)}) collective-permute-start(bf16[3,2048,2]{1,2,0:T(2,128)(2,1)S(1)} %slice.45), channel_id=1, source_target_pairs={{0,4},{4,8},{8,12},{12,16},{16,20},{20,24},{24,28},{28,32},{32,36}... | collective-permute-start | bytes 73736 | tf_op jit(solution)/shard_map/ppermute | solution.py:279
  49.7 8.3 %copy-start.2 = (bf16[3,2048,128]{2,1,0:T(8,128)(2,1)S(1)}, bf16[3,2048,128]{2,1,0:T(8,128)(2,1)}, u32[]{:S(2)}) copy-start(bf16[3,2048,128]{2,1,0:T(8,128)(2,1)} %value_ref.1) | copy-start | bytes 4718596
  49.7 27.0 %all-to-all-start.1 = ((bf16[128,16,128]{2,1,0:T(8,128)(2,1)}), bf16[128,16,128]{2,1,0:T(8,128)(2,1)S(1)}, u32[]{:S(2)}, u32[]{:S(2)}) async-start(bf16[128,16,128]{2,1,0:T(8,128)(2,1)} %bitcast.2), calls=%async_computation.1 | async-start | bytes 1048576 | tf_op jit(solution)/shard_map/all_to_all | solution.py:281
  65.2 0.7 copy-start.4
  65.2 1.0 %copy-start.5 = (f32[2048]{0:T(1024)S(1)}, f32[2048]{0:T(1024)}, u32[]{:S(2)}) copy-start(f32[2048]{0:T(1024)} %param.9) | copy-start | bytes 24580

commit v5 on v4

--- a/solution.py
+++ b/solution.py
@@ -25,11 +25,18 @@
 def pack_product(streams, short_weight, filters, owned):
     taps, _, chan = short_weight.shape
     owners = chan // owned
-    chunk = 1024
+    parts = 2
+    chunk = chan // parts
     per = chunk // owned
     terms = 2 * taps
 
-    def kernel(key_ref, value_ref, weight_ref, filt_ref, out_ref):
+    def kernel(streams_in, weight_in, filt_in, out_ref, raw_ref, weight_ref, filt_ref, pack_ref, sems, out_sems):
+        weight_copy = pltpu.make_async_copy(weight_in, weight_ref, sems.at[0])
+        raw_copy = pltpu.make_async_copy(streams_in.at[pl.ds(1, 2)], raw_ref, sems.at[1])
+        filt_copy = pltpu.make_async_copy(filt_in, filt_ref, sems.at[2])
+        weight_copy.start()
+        raw_copy.start()
+        filt_copy.start()
         src = row_iota((LANES, LANES))
         place = lane_iota((LANES, LANES)) // owned
         pick = []
@@ -39,55 +46,66 @@
                 hit = jnp.where((place == 4 * stream + n) & (src == pos), 1.0, hit)
             pick.append(hit)
         pick = jnp.concatenate(pick, axis=0).astype(bf16)
-        weight = weight_ref[...].reshape(3 * taps, chunk)
-        high = weight.astype(bf16).astype(f32)
-        middle = (weight - high).astype(bf16).astype(f32)
-        parts = [high, middle, weight - high - middle, jnp.zeros((32 - 9 * taps, chunk), f32)]
-        parts = jnp.transpose(jnp.concatenate(parts, axis=0)).astype(bf16)
         row = row_iota((32, terms * LANES))
         block = lane_iota((32, terms * LANES)) // LANES
         wanted = 3 * (block % taps) + block // taps + 1
         choose = jnp.where((row % (3 * taps) == wanted) & (row < 9 * taps), 1.0, 0.0).astype(bf16)
-        along = jnp.dot(parts, choose, preferred_element_type=f32)
-        part = chunk // 2
-        shape = (part, LANES)
+        shape = (chunk, LANES)
         inner = lane_iota(shape) >= taps - 1
         same = lane_iota(shape) % owned == row_iota(shape) % owned
-        for begin in range(0, chunk, part):
-            rows = slice(begin, begin + part)
-            own = slice(begin // owned, (begin + part) // owned)
-            along = jnp.dot(parts[rows], choose, preferred_element_type=f32)
+        weight_copy.wait()
+        weight = 0.5 * weight_ref[...].reshape(3 * taps, chan)
+        high = weight.astype(bf16).astype(f32)
+        middle = (weight - high).astype(bf16).astype(f32)
+        split = [high, middle, weight - high - middle, jnp.zeros((32 - 9 * taps, chan), f32)]
+        split = jnp.transpose(jnp.concatenate(split, axis=0)).astype(bf16)
+        raw_copy.wait()
+        filt_copy.wait()
+        copies = []
+        for part in range(parts):
+            rows = slice(part * chunk, (part + 1) * chunk)
+            own = slice(part * per, (part + 1) * per)
+            along = jnp.dot(split[rows], choose, preferred_element_type=f32)
             convs = []
-            for stream, raw_ref in enumerate((key_ref, value_ref)):
-                raw = raw_ref[0, rows]
+            for stream in range(2):
+                raw = raw_ref[stream, rows]
                 total = along[:, stream * taps * LANES : (stream * taps + 1) * LANES] * raw.astype(f32)
                 for j in range(1, taps):
                     at = (stream * taps + j) * LANES
                     total = total + along[:, at : at + LANES] * pltpu.roll(raw, j, 1).astype(f32)
-                convs.append(total)
+                convs.append(total + total)
             product = jnp.where(inner, convs[0] * convs[1], 0.0).astype(bf16)
-            out_ref[own, 0 : owned // 2] = product.reshape(part // owned, owned // 2, 2, LANES)
-            both = jnp.concatenate([key_ref[0, rows], value_ref[0, rows]], axis=1)
+            pack_ref[own, 0 : owned // 2] = product.reshape(per, owned // 2, 2, LANES)
+            both = jnp.concatenate([raw_ref[0, rows], raw_ref[1, rows]], axis=1)
             spread = jnp.where(same, jnp.dot(both, pick, preferred_element_type=f32), 0.0)
-            ends = jnp.sum(spread.reshape(part // owned, owned, LANES), axis=1)
-            first = row_iota((part // owned, 2, LANES)) == 0
+            ends = jnp.sum(spread.reshape(per, owned, LANES), axis=1)
+            first = row_iota((per, 2, LANES)) == 0
             rest = jnp.where(first, filt_ref[own][:, None, :], ends[:, None, :])
-            out_ref[own, owned // 2] = rest.astype(bf16)
-
+            pack_ref[own, owned // 2] = rest.astype(bf16)
+            where = pl.ds(part * per, per)
+            copies.append(pltpu.make_async_copy(pack_ref.at[where], out_ref.at[where], out_sems.at[part]))
+            copies[part].start()
+        for copy in copies:
+            copy.wait()
+
+    hbm = pl.BlockSpec(memory_space=pltpu.HBM)
+    packed = (owners, owned // 2 + 1, 2, LANES)
     return pl.pallas_call(
         kernel,
-        grid=(chan // chunk,),
-        out_shape=jax.ShapeDtypeStruct((owners, owned // 2 + 1, 2, LANES), bf16),
-        in_specs=[
-            pl.BlockSpec((1, chunk, LANES), lambda i: (1, i, 0)),
-            pl.BlockSpec((1, chunk, LANES), lambda i: (2, i, 0)),
-            pl.BlockSpec((taps, 3, chunk), lambda i: (0, 0, i)),
-            pl.BlockSpec((per, LANES), lambda i: (i, 0)),
+        out_shape=jax.ShapeDtypeStruct(packed, bf16),
+        in_specs=[hbm, hbm, hbm],
+        out_specs=hbm,
+        scratch_shapes=[
+            pltpu.VMEM((2, chan, LANES), bf16),
+            pltpu.VMEM((taps, 3, chan), f32),
+            pltpu.VMEM((owners, LANES), f32),
+            pltpu.VMEM(packed, bf16),
+            pltpu.SemaphoreType.DMA((3,)),
+            pltpu.SemaphoreType.DMA((parts,)),
         ],
-        out_specs=pl.BlockSpec((per, owned // 2 + 1, 2, LANES), lambda i: (i, 0, 0, 0)),
         compiler_params=pltpu.CompilerParams(vmem_limit_bytes=32 << 20),
         name="pack_product",
-    )(*(pltpu.with_memory_space_constraint(x, pltpu.HBM) for x in (streams, streams, short_weight, filters)))
+    )(*(pltpu.with_memory_space_constraint(x, pltpu.HBM) for x in (streams, short_weight, filters)))
 
 
 def end_terms(owned):
@@ -148,7 +166,6 @@
                     size = min(chunk, rows - top)
                     left = lag * wide + parity * LANES
                     cols_ref[top : top + size, left : left + LANES] = part[0:size]
-        acc_ref[...] = jnp.zeros_like(acc_ref)
         upper = dst >= src
         toep_ref[0] = jnp.zeros((LANES, LANES), bf16)
 
@@ -169,9 +186,11 @@
                 parts.append(jnp.concatenate([toep_ref[2 * lag + 1], toep_ref[2 * lag + 2]], axis=1))
                 parts.append(jnp.concatenate([toep_ref[2 * lag], toep_ref[2 * lag + 1]], axis=1))
             start = step * span * owned
-            acc_ref[start:rows, :] += jnp.dot(
-                cols_ref[0 : rows - start, :], jnp.concatenate(parts, axis=0), preferred_element_type=f32
-            )
+            added = jnp.dot(cols_ref[0 : rows - start, :], jnp.concatenate(parts, axis=0), preferred_element_type=f32)
+            if step:
+                acc_ref[start:rows, :] += added
+            else:
+                acc_ref[...] = added
         out_ref[:, 0] = acc_ref[:, 0:LANES].astype(bf16).reshape(half, owned, LANES)
         out_ref[:, 1] = acc_ref[:, LANES:wide].astype(bf16).reshape(half, owned, LANES)
 
@@ -237,7 +256,7 @@
 def finish(gated, squares, count):
     chan, length = gated.shape
 
-    parts = 4
+    parts = 2
     chunk = chan // parts
 
     def kernel(gated_ref, squares_ref, out_ref, done_ref, sems):

time: 88 us -> 87.8 us (level)
  no operation moved by 1% of the time
where the time goes in v5:
time: 87.8 us; the launch traced here: 87.5 us
  waiting for transfers between devices  26.9 us (31%)
  starting transfers between devices  26.1 us (30%)
  Pallas kernels  11.5 us (13%)
  blocking collectives  9.67 us (11%)
  other arithmetic  7.65 us (9%)
  local copies, waits for them, and re-layouts  5.29 us (6%)
    all_to_all x1, starting transfers between devices, shards(): recv = lax.all_to_all(send, 'ctx', 0, 0)  17.4 us
    all_to_all x1, waiting for transfers between devices, shards(): recv = lax.all_to_all(send, 'ctx', 0, 0)  16.9 us
    all_to_all x1, waiting for transfers between devices, shards(): back = lax.all_to_all(mixed, 'ctx', 0, 0).reshape(local_chan, length)  10 us
    all_gather x1, blocking collectives, shards(): return finish(gated, lax.all_gather(squares, 'tp'), local_chan * n_width)  9.67 us
    all_to_all x1, starting transfers between devices, shards(): back = lax.all_to_all(mixed, 'ctx', 0, 0).reshape(local_chan, length)  6.67 us
    pallas_call x1, Pallas kernels, long_conv_blocks(): pl.pallas_call(kernel, out_shape=jax.ShapeDtypeStruct((half, 2, owned, LA...  6.63 us
    add x1, other arithmetic, local_streams(): conv + short_weight[offset][:, :, None] * padded[:, :, start:start + length]  4.67 us
    pallas_call x1, Pallas kernels, pack_product(): pl.pallas_call(kernel, out_shape=jax.ShapeDtypeStruct(packed, bf16), in_s...  3.76 us
  transfers between devices with their start and end apart: 3, of which 2 were waited for; matrix products, arithmetic and copies ran while one was open for 14% of the time, Pallas kernels for 8%

profile of v5, /device:TPU:8, one launch (start us, length us, event | category | flops | bytes accessed | tf_op | source)
XLA Modules:
  0.0 87.5 jit_solution(14294256094238718031)
XLA Ops:
  0.0 0.0 copy-start
  0.0 0.0 copy-start.3
  0.0 3.8 %pack_product.1 = bf16[128,9,2,128]{3,2,1,0:T(2,128)(2,1)} custom-call(bf16[3,2048,128]{2,1,0:T(8,128)(2,1)} %streams_in.1, f32[3,3,2048]{2,1,0:T(4,128)} %weight_in.1, f32[128,128]{1,0:T(8,128)} %filt_in.1), custom_call_target="tpu_custom_call" | custom-call | tf_op jit(solution)/shard_map/pack_product/pallas_call | solution.py:93
  3.8 17.4 %all-to-all-start = ((bf16[128,9,2,128]{3,2,1,0:T(2,128)(2,1)}), bf16[128,9,2,128]{3,2,1,0:T(2,128)(2,1)S(1)}, u32[]{:S(2)}, u32[]{:S(2)}) async-start(bf16[128,9,2,128]{3,2,1,0:T(2,128)(2,1)} %pack_product.1), calls=%async_computation | async-start | bytes 1179648 | tf_op jit(solution)/shard_map/all_to_all | solution.py:293
  21.2 0.0 copy-done.1
  21.2 1.6 %copy.9 = bf16[3,2048,128]{1,2,0:T(8,128)(2,1)} copy(bf16[3,2048,128]{2,1,0:T(8,128)(2,1)S(1)} %copy-done.1) | data formatting | bytes 3145728 | tf_op jit(solution)/shard_map/optimization_barrier | solution.py:294
  22.8 0.9 %slice.45 = bf16[3,2048,2]{1,2,0:T(2,128)(2,1)S(1)} slice(bf16[3,2048,128]{1,2,0:T(8,128)(2,1)} %copy.9), slice={[0:3], [0:2048], [126:128]} | slice | bytes 49152 | tf_op jit(solution)/shard_map/slice | solution.py:298
  23.7 2.1 %collective-permute-start = (bf16[3,2048,2]{1,2,0:T(2,128)(2,1)S(1)}, bf16[3,2048,2]{1,2,0:T(2,128)(2,1)S(1)}, u32[]{:S(2)}, u32[]{:S(2)}) collective-permute-start(bf16[3,2048,2]{1,2,0:T(2,128)(2,1)S(1)} %slice.45), channel_id=1, source_target_pairs={{0,4},{4,8},{8,12},{12,16},{16,20},{20,24},{24,28},{28,32},{32,36}... | collective-permute-start | bytes 73736 | tf_op jit(solution)/shard_map/ppermute | solution.py:298
  25.8 0.0 copy-done.3
  25.8 0.1 dynamic-slice_bitcast_fusion
  25.9 0.1 tile.12
  26.0 16.9 %all-to-all-done = bf16[128,9,2,128]{3,2,1,0:T(2,128)(2,1)S(1)} async-done(((bf16[128,9,2,128]{3,2,1,0:T(2,128)(2,1)}), bf16[128,9,2,128]{3,2,1,0:T(2,128)(2,1)S(1)}, u32[]{:S(2)}, u32[]{:S(2)}) %all-to-all-start) | async-done | bytes 589856 | tf_op jit(solution)/shard_map/all_to_all | solution.py:293
  42.9 0.0 copy-done
  42.9 6.6 %long_conv.1 = bf16[64,2,16,128]{3,2,1,0:T(8,128)(2,1)} custom-call(bf16[64,2,9,2,128]{4,3,2,1,0:T(2,128)(2,1)S(1)} %bitcast.16, f32[8,128]{1,0:T(8,128)S(1)} %pad.4.weight_ref, bf16[256,768]{1,0:T(8,128)(2,1)S(1)} %copy-done), custom_call_target="tpu_custom_call" | custom-call | tf_op jit(solution)/shard_map/long_conv/pallas_call | solution.py:198
  49.5 6.7 %all-to-all-start.1 = ((bf16[128,16,128]{2,1,0:T(8,128)(2,1)}), bf16[128,16,128]{2,1,0:T(8,128)(2,1)S(1)}, u32[]{:S(2)}, u32[]{:S(2)}) async-start(bf16[128,16,128]{2,1,0:T(8,128)(2,1)} %bitcast.2), calls=%async_computation.1 | async-start | bytes 1048576 | tf_op jit(solution)/shard_map/all_to_all | solution.py:300
  56.2 0.0 collective-permute-done
  56.2 1.6 %copy.11 = bf16[3,2048,2]{2,1,0:T(8,128)(2,1)} copy(bf16[3,2048,2]{1,2,0:T(2,128)(2,1)S(1)} %collective-permute-done) | data formatting | bytes 49152 | tf_op jit(solution)/shard_map/optimization_barrier | solution.py:301
  57.8 0.0 copy-done.2
  57.8 2.5 %maximum_convert_fusion = f32[3,2048,130]{2,1,0:T(8,128)S(1)} fusion(bf16[3,2048,128]{2,1,0:T(8,128)(2,1)S(1)} %copy-done.2, bf16[3,2048,2]{2,1,0:T(8,128)(2,1)} %copy.11), kind=kLoop, calls=%fused_computation.5 | loop fusion | flops 3194880 | bytes 4792320 | tf_op jit(solution)/shard_map/convert_element_type | solution.py:219
  60.4 4.7 %fusion = f32[3,2048,128]{2,1,0:T(8,128)S(1)} fusion(f32[3,2048,130]{2,1,0:T(8,128)S(1)} %maximum_convert_fusion, f32[3,2048]{1,0:T(4,128)S(1)} %get-tuple-element.40, f32[3,2048]{1,0:T(4,128)S(1)} %get-tuple-element.41, f32[3,2048]{1,0:T(4,128)S(1)} %get-tuple-element.39), kind=kLoop, calls=%fused_computation.1 | loop fusion | flops 3932160 | bytes 12656640 | tf_op jit(solution)/shard_map/add | solution.py:223
  65.1 0.0 copy-start.4
  65.1 0.0 copy-start.5
  65.1 0.1 fusion.3.query_ref
  65.2 0.1 fusion.4
  65.3 0.5 copy-done.4
  65.8 0.3 broadcast_in_dim.2.gain_ref
  66.1 0.0 copy-done.5
  66.1 0.3 convert_multiply_fusion.direct_ref
  66.4 10.0 %all-to-all-done.1 = bf16[128,16,128]{2,1,0:T(8,128)(2,1)S(1)} async-done(((bf16[128,16,128]{2,1,0:T(8,128)(2,1)}), bf16[128,16,128]{2,1,0:T(8,128)(2,1)S(1)}, u32[]{:S(2)}, u32[]{:S(2)}) %all-to-all-start.1) | async-done | bytes 524320 | tf_op jit(solution)/shard_map/all_to_all | solution.py:300
  76.5 0.3 gate.1
  76.8 9.7 %all-gather.1.squares_ref = f32[4,1,128]{2,1,0:T(1,128)S(1)} all-gather(f32[1,1,128]{2,1,0:T(1,128)S(1)} %bitcast.18), channel_id=2, replica_groups=mesh['ctx'=128,'tp'=4] {'tp'}, dimensions={0}, use_global_device_ids=true | all-gather | bytes 2560 | tf_op jit(solution)/shard_map/all_gather | solution.py:310
  86.5 0.9 finish.1
  (7 shorter events, 0.1 us)
Async XLA Ops:
  0.0 42.9 %copy-start = (bf16[256,768]{1,0:T(8,128)(2,1)S(1)}, bf16[256,768]{1,0:T(8,128)(2,1)}, u32[]{:S(2)}) copy-start(bf16[256,768]{1,0:T(8,128)(2,1)} %constant.16.clone.terms_ref) | copy-start | bytes 1179652
  0.0 21.2 %copy-start.1 = (bf16[3,2048,128]{2,1,0:T(8,128)(2,1)S(1)}, bf16[3,2048,128]{2,1,0:T(8,128)(2,1)}, u32[]{:S(2)}) copy-start(bf16[3,2048,128]{2,1,0:T(8,128)(2,1)} %streams_in.1) | copy-start | bytes 4718596
  0.0 25.8 %copy-start.3 = (f32[3,3,2048]{2,1,0:T(4,128)S(1)}, f32[3,3,2048]{2,1,0:T(4,128)}, u32[]{:S(2)}) copy-start(f32[3,3,2048]{2,1,0:T(4,128)} %weight_in.1) | copy-start | bytes 221188
  3.8 39.1 %all-to-all-start = ((bf16[128,9,2,128]{3,2,1,0:T(2,128)(2,1)}), bf16[128,9,2,128]{3,2,1,0:T(2,128)(2,1)S(1)}, u32[]{:S(2)}, u32[]{:S(2)}) async-start(bf16[128,9,2,128]{3,2,1,0:T(2,128)(2,1)} %pack_product.1), calls=%async_computation | async-start | bytes 1179648 | tf_op jit(solution)/shard_map/all_to_all | solution.py:293
  23.7 32.4 %collective-permute-start = (bf16[3,2048,2]{1,2,0:T(2,128)(2,1)S(1)}, bf16[3,2048,2]{1,2,0:T(2,128)(2,1)S(1)}, u32[]{:S(2)}, u32[]{:S(2)}) collective-permute-start(bf16[3,2048,2]{1,2,0:T(2,128)(2,1)S(1)} %slice.45), channel_id=1, source_target_pairs={{0,4},{4,8},{8,12},{12,16},{16,20},{20,24},{24,28},{28,32},{32,36}... | collective-permute-start | bytes 73736 | tf_op jit(solution)/shard_map/ppermute | solution.py:298
  49.5 8.3 %copy-start.2 = (bf16[3,2048,128]{2,1,0:T(8,128)(2,1)S(1)}, bf16[3,2048,128]{2,1,0:T(8,128)(2,1)}, u32[]{:S(2)}) copy-start(bf16[3,2048,128]{2,1,0:T(8,128)(2,1)} %streams_in.1) | copy-start | bytes 4718596
  49.5 27.0 %all-to-all-start.1 = ((bf16[128,16,128]{2,1,0:T(8,128)(2,1)}), bf16[128,16,128]{2,1,0:T(8,128)(2,1)S(1)}, u32[]{:S(2)}, u32[]{:S(2)}) async-start(bf16[128,16,128]{2,1,0:T(8,128)(2,1)} %bitcast.2), calls=%async_computation.1 | async-start | bytes 1048576 | tf_op jit(solution)/shard_map/all_to_all | solution.py:300
  65.1 0.7 copy-start.4
  65.1 1.0 %copy-start.5 = (f32[2048]{0:T(1024)S(1)}, f32[2048]{0:T(1024)}, u32[]{:S(2)}) copy-start(f32[2048]{0:T(1024)} %param.9) | copy-start | bytes 24580

commit v6 on v5

--- a/solution.py
+++ b/solution.py
@@ -124,9 +124,8 @@
     blocks = recv.shape[0]
     half = blocks // 2
     rows = half * owned
-    span = 2
     wide = 2 * LANES
-    chunk = 256
+    chunk = 512
 
     def kernel(recv_ref, weight_ref, terms_ref, out_ref, toep_ref, cols_ref, acc_ref, ends_ref, first_ref):
         for k in range(blocks):
@@ -148,10 +147,9 @@
         src = row_iota((LANES, LANES))
         dst = lane_iota((LANES, LANES))
         to_lane = jnp.where((src // owned == dst) & (dst < 2), 1.0, 0.0).astype(bf16)
-        for lag in range(1, span):
-            cols_ref[0 : lag * owned, lag * wide : (lag + 1) * wide] = jnp.zeros((lag * owned, wide), bf16)
-        for parity in range(2):
-            for begin in range(0, rows, chunk):
+
+        def place(begin):
+            for parity in range(2):
                 spread = []
                 for pair in range(begin // owned, (begin + chunk) // owned):
                     block = 2 * pair + parity
@@ -161,36 +159,39 @@
                 patch = jnp.dot(spread, to_lane, preferred_element_type=f32)
                 part = recv_ref[begin // owned : (begin + chunk) // owned, parity, 0 : owned // 2]
                 part = (part.reshape(chunk, LANES).astype(f32) + patch).astype(bf16)
-                for lag in range(span):
-                    top = begin + lag * owned
-                    size = min(chunk, rows - top)
-                    left = lag * wide + parity * LANES
-                    cols_ref[top : top + size, left : left + LANES] = part[0:size]
+                cols_ref[begin : begin + chunk, parity * LANES : (parity + 1) * LANES] = part
+
         upper = dst >= src
         toep_ref[0] = jnp.zeros((LANES, LANES), bf16)
 
-        def build(first, count, before):
-            for k in range(first, first + count):
-                taps = recv_ref[k // 2, k % 2, owned // 2].astype(f32)[0:1]
-                turned = pltpu.roll(jnp.broadcast_to(taps, (LANES, LANES)), 0, 1, stride=1, stride_axis=0)
+        def turn(k):
+            taps = recv_ref[k // 2, k % 2, owned // 2].astype(f32)[0:1]
+            return pltpu.roll(jnp.broadcast_to(taps, (LANES, LANES)), 0, 1, stride=1, stride_axis=0)
+
+        def build(last, count, turned):
+            for k in range(last, last - count, -1):
+                before = turn(k - 1) if k else jnp.zeros((LANES, LANES), f32)
                 toep_ref[k + 1] = jnp.where(upper, turned, before).astype(bf16)
-                before = turned
-            return before
-
-        before = build(0, 2 * span, jnp.zeros((LANES, LANES), f32))
-        for step in range(half // span):
-            if (step + 1) * span < half:
-                before = build((step + 1) * 2 * span, 2 * span, before)
-            parts = []
-            for lag in range(step * span, (step + 1) * span):
-                parts.append(jnp.concatenate([toep_ref[2 * lag + 1], toep_ref[2 * lag + 2]], axis=1))
-                parts.append(jnp.concatenate([toep_ref[2 * lag], toep_ref[2 * lag + 1]], axis=1))
-            start = step * span * owned
-            added = jnp.dot(cols_ref[0 : rows - start, :], jnp.concatenate(parts, axis=0), preferred_element_type=f32)
-            if step:
-                acc_ref[start:rows, :] += added
-            else:
-                acc_ref[...] = added
+                turned = before
+            return turned
+
+        turned = turn(blocks - 1)
+        turned = build(blocks - 1, 3, turned)
+        ready = 0
+        for lag in reversed(range(half)):
+            start = lag * owned
+            while ready < rows - start:
+                place(ready)
+                ready += chunk
+            if lag:
+                turned = build(2 * lag - 2, 2 if lag > 1 else 1, turned)
+            even = jnp.concatenate([toep_ref[2 * lag + 1], toep_ref[2 * lag + 2]], axis=1)
+            odd = jnp.concatenate([toep_ref[2 * lag], toep_ref[2 * lag + 1]], axis=1)
+            weights = jnp.concatenate([even, odd], axis=0)
+            added = jnp.dot(cols_ref[0 : rows - start, :], weights, preferred_element_type=f32)
+            acc_ref[start : start + owned, :] = added[0:owned]
+            if lag + 1 < half:
+                acc_ref[start + owned : rows, :] += added[owned:]
         out_ref[:, 0] = acc_ref[:, 0:LANES].astype(bf16).reshape(half, owned, LANES)
         out_ref[:, 1] = acc_ref[:, LANES:wide].astype(bf16).reshape(half, owned, LANES)
 
@@ -202,7 +203,7 @@
         out_specs=vmem,
         scratch_shapes=[
             pltpu.VMEM((blocks + 1, LANES, LANES), bf16),
-            pltpu.VMEM((rows, span * wide), bf16),
+            pltpu.VMEM((rows, wide), bf16),
             pltpu.VMEM((rows, wide), f32),
             pltpu.VMEM((blocks, LANES), f32),
             pltpu.VMEM((blocks, LANES), f32),

time: 87.8 us -> 87.3 us (level)
  transfers between devices with their start and end apart: 3 -> 3, of which waited for: 2 -> 2; matrix products, arithmetic and copies ran while one was open for 14% -> 14% of each run, Pallas kernels for 8% -> 7%
where the time goes in v6:
time: 87.3 us; the launch traced here: 87 us
  waiting for transfers between devices  26.9 us (31%)
  starting transfers between devices  26.1 us (30%)
  Pallas kernels  11.1 us (13%)
  blocking collectives  9.67 us (11%)
  other arithmetic  7.65 us (9%)
  local copies, waits for them, and re-layouts  5.29 us (6%)
    all_to_all x1, starting transfers between devices, shards(): recv = lax.all_to_all(send, 'ctx', 0, 0)  17.4 us
    all_to_all x1, waiting for transfers between devices, shards(): recv = lax.all_to_all(send, 'ctx', 0, 0)  16.9 us
    all_to_all x1, waiting for transfers between devices, shards(): back = lax.all_to_all(mixed, 'ctx', 0, 0).reshape(local_chan, length)  10 us
    all_gather x1, blocking collectives, shards(): return finish(gated, lax.all_gather(squares, 'tp'), local_chan * n_width)  9.67 us
    all_to_all x1, starting transfers between devices, shards(): back = lax.all_to_all(mixed, 'ctx', 0, 0).reshape(local_chan, length)  6.67 us
    pallas_call x1, Pallas kernels, long_conv_blocks(): pl.pallas_call(kernel, out_shape=jax.ShapeDtypeStruct((half, 2, owned, LA...  6.14 us
    add x1, other arithmetic, local_streams(): conv + short_weight[offset][:, :, None] * padded[:, :, start:start + length]  4.67 us
    pallas_call x1, Pallas kernels, pack_product(): pl.pallas_call(kernel, out_shape=jax.ShapeDtypeStruct(packed, bf16), in_s...  3.76 us
  transfers between devices with their start and end apart: 3, of which 2 were waited for; matrix products, arithmetic and copies ran while one was open for 14% of the time, Pallas kernels for 7%

profile of v6, /device:TPU:8, one launch (start us, length us, event | category | flops | bytes accessed | tf_op | source)
XLA Modules:
  0.0 87.0 jit_solution(1202600581755523846)
XLA Ops:
  0.0 0.0 copy-start
  0.0 0.0 copy-start.1
  0.0 3.8 %pack_product.1 = bf16[128,9,2,128]{3,2,1,0:T(2,128)(2,1)} custom-call(bf16[3,2048,128]{2,1,0:T(8,128)(2,1)} %streams_in.1, f32[3,3,2048]{2,1,0:T(4,128)} %weight_in.1, f32[128,128]{1,0:T(8,128)} %filt_in.1), custom_call_target="tpu_custom_call" | custom-call | tf_op jit(solution)/shard_map/pack_product/pallas_call | solution.py:93
  3.8 17.4 %all-to-all-start = ((bf16[128,9,2,128]{3,2,1,0:T(2,128)(2,1)}), bf16[128,9,2,128]{3,2,1,0:T(2,128)(2,1)S(1)}, u32[]{:S(2)}, u32[]{:S(2)}) async-start(bf16[128,9,2,128]{3,2,1,0:T(2,128)(2,1)} %pack_product.1), calls=%async_computation | async-start | bytes 1179648 | tf_op jit(solution)/shard_map/all_to_all | solution.py:294
  21.2 0.0 copy-done.1
  21.2 1.6 %copy.9 = bf16[3,2048,128]{1,2,0:T(8,128)(2,1)} copy(bf16[3,2048,128]{2,1,0:T(8,128)(2,1)S(1)} %copy-done.1) | data formatting | bytes 3145728 | tf_op jit(solution)/shard_map/optimization_barrier | solution.py:295
  22.8 0.9 %slice.45 = bf16[3,2048,2]{1,2,0:T(2,128)(2,1)S(1)} slice(bf16[3,2048,128]{1,2,0:T(8,128)(2,1)} %copy.9), slice={[0:3], [0:2048], [126:128]} | slice | bytes 49152 | tf_op jit(solution)/shard_map/slice | solution.py:299
  23.7 2.1 %collective-permute-start = (bf16[3,2048,2]{1,2,0:T(2,128)(2,1)S(1)}, bf16[3,2048,2]{1,2,0:T(2,128)(2,1)S(1)}, u32[]{:S(2)}, u32[]{:S(2)}) collective-permute-start(bf16[3,2048,2]{1,2,0:T(2,128)(2,1)S(1)} %slice.45), channel_id=1, source_target_pairs={{0,4},{4,8},{8,12},{12,16},{16,20},{20,24},{24,28},{28,32},{32,36}... | collective-permute-start | bytes 73736 | tf_op jit(solution)/shard_map/ppermute | solution.py:299
  25.8 0.0 copy-done.3
  25.8 0.1 dynamic-slice_bitcast_fusion
  25.9 0.1 tile.12
  26.0 16.9 %all-to-all-done = bf16[128,9,2,128]{3,2,1,0:T(2,128)(2,1)S(1)} async-done(((bf16[128,9,2,128]{3,2,1,0:T(2,128)(2,1)}), bf16[128,9,2,128]{3,2,1,0:T(2,128)(2,1)S(1)}, u32[]{:S(2)}, u32[]{:S(2)}) %all-to-all-start) | async-done | bytes 589856 | tf_op jit(solution)/shard_map/all_to_all | solution.py:294
  42.9 0.0 copy-done
  42.9 6.1 %long_conv.1 = bf16[64,2,16,128]{3,2,1,0:T(8,128)(2,1)} custom-call(bf16[64,2,9,2,128]{4,3,2,1,0:T(2,128)(2,1)S(1)} %bitcast.16, f32[8,128]{1,0:T(8,128)S(1)} %pad.4.weight_ref, bf16[256,768]{1,0:T(8,128)(2,1)S(1)} %copy-done), custom_call_target="tpu_custom_call" | custom-call | tf_op jit(solution)/shard_map/long_conv/pallas_call | solution.py:199
  49.0 6.7 %all-to-all-start.1 = ((bf16[128,16,128]{2,1,0:T(8,128)(2,1)}), bf16[128,16,128]{2,1,0:T(8,128)(2,1)S(1)}, u32[]{:S(2)}, u32[]{:S(2)}) async-start(bf16[128,16,128]{2,1,0:T(8,128)(2,1)} %bitcast.2), calls=%async_computation.1 | async-start | bytes 1048576 | tf_op jit(solution)/shard_map/all_to_all | solution.py:301
  55.7 0.0 collective-permute-done
  55.7 1.6 %copy.11 = bf16[3,2048,2]{2,1,0:T(8,128)(2,1)} copy(bf16[3,2048,2]{1,2,0:T(2,128)(2,1)S(1)} %collective-permute-done) | data formatting | bytes 49152 | tf_op jit(solution)/shard_map/optimization_barrier | solution.py:302
  57.3 0.0 copy-done.2
  57.4 2.5 %maximum_convert_fusion = f32[3,2048,130]{2,1,0:T(8,128)S(1)} fusion(bf16[3,2048,128]{2,1,0:T(8,128)(2,1)S(1)} %copy-done.2, bf16[3,2048,2]{2,1,0:T(8,128)(2,1)} %copy.11), kind=kLoop, calls=%fused_computation.5 | loop fusion | flops 3194880 | bytes 4792320 | tf_op jit(solution)/shard_map/convert_element_type | solution.py:220
  59.9 4.7 %fusion = f32[3,2048,128]{2,1,0:T(8,128)S(1)} fusion(f32[3,2048,130]{2,1,0:T(8,128)S(1)} %maximum_convert_fusion, f32[3,2048]{1,0:T(4,128)S(1)} %get-tuple-element.40, f32[3,2048]{1,0:T(4,128)S(1)} %get-tuple-element.41, f32[3,2048]{1,0:T(4,128)S(1)} %get-tuple-element.39), kind=kLoop, calls=%fused_computation.1 | loop fusion | flops 3932160 | bytes 12656640 | tf_op jit(solution)/shard_map/add | solution.py:224
  64.6 0.0 copy-start.4
  64.6 0.0 copy-start.5
  64.6 0.1 fusion.3.query_ref
  64.7 0.1 fusion.4
  64.8 0.5 copy-done.4
  65.3 0.3 broadcast_in_dim.2.gain_ref
  65.6 0.0 copy-done.5
  65.6 0.3 convert_multiply_fusion.direct_ref
  66.0 10.0 %all-to-all-done.1 = bf16[128,16,128]{2,1,0:T(8,128)(2,1)S(1)} async-done(((bf16[128,16,128]{2,1,0:T(8,128)(2,1)}), bf16[128,16,128]{2,1,0:T(8,128)(2,1)S(1)}, u32[]{:S(2)}, u32[]{:S(2)}) %all-to-all-start.1) | async-done | bytes 524320 | tf_op jit(solution)/shard_map/all_to_all | solution.py:301
  76.0 0.3 gate.1
  76.3 9.7 %all-gather.1.squares_ref = f32[4,1,128]{2,1,0:T(1,128)S(1)} all-gather(f32[1,1,128]{2,1,0:T(1,128)S(1)} %bitcast.18), channel_id=2, replica_groups=mesh['ctx'=128,'tp'=4] {'tp'}, dimensions={0}, use_global_device_ids=true | all-gather | bytes 2560 | tf_op jit(solution)/shard_map/all_gather | solution.py:311
  86.0 0.9 finish.1
  (7 shorter events, 0.1 us)
Async XLA Ops:
  0.0 42.9 %copy-start = (bf16[256,768]{1,0:T(8,128)(2,1)S(1)}, bf16[256,768]{1,0:T(8,128)(2,1)}, u32[]{:S(2)}) copy-start(bf16[256,768]{1,0:T(8,128)(2,1)} %constant.16.clone.terms_ref) | copy-start | bytes 1179652
  0.0 21.2 %copy-start.1 = (bf16[3,2048,128]{2,1,0:T(8,128)(2,1)S(1)}, bf16[3,2048,128]{2,1,0:T(8,128)(2,1)}, u32[]{:S(2)}) copy-start(bf16[3,2048,128]{2,1,0:T(8,128)(2,1)} %streams_in.1) | copy-start | bytes 4718596
  0.0 25.8 %copy-start.3 = (f32[3,3,2048]{2,1,0:T(4,128)S(1)}, f32[3,3,2048]{2,1,0:T(4,128)}, u32[]{:S(2)}) copy-start(f32[3,3,2048]{2,1,0:T(4,128)} %weight_in.1) | copy-start | bytes 221188
  3.8 39.1 %all-to-all-start = ((bf16[128,9,2,128]{3,2,1,0:T(2,128)(2,1)}), bf16[128,9,2,128]{3,2,1,0:T(2,128)(2,1)S(1)}, u32[]{:S(2)}, u32[]{:S(2)}) async-start(bf16[128,9,2,128]{3,2,1,0:T(2,128)(2,1)} %pack_product.1), calls=%async_computation | async-start | bytes 1179648 | tf_op jit(solution)/shard_map/all_to_all | solution.py:294
  23.7 31.9 %collective-permute-start = (bf16[3,2048,2]{1,2,0:T(2,128)(2,1)S(1)}, bf16[3,2048,2]{1,2,0:T(2,128)(2,1)S(1)}, u32[]{:S(2)}, u32[]{:S(2)}) collective-permute-start(bf16[3,2048,2]{1,2,0:T(2,128)(2,1)S(1)} %slice.45), channel_id=1, source_target_pairs={{0,4},{4,8},{8,12},{12,16},{16,20},{20,24},{24,28},{28,32},{32,36}... | collective-permute-start | bytes 73736 | tf_op jit(solution)/shard_map/ppermute | solution.py:299
  49.0 8.3 %copy-start.2 = (bf16[3,2048,128]{2,1,0:T(8,128)(2,1)S(1)}, bf16[3,2048,128]{2,1,0:T(8,128)(2,1)}, u32[]{:S(2)}) copy-start(bf16[3,2048,128]{2,1,0:T(8,128)(2,1)} %streams_in.1) | copy-start | bytes 4718596
  49.0 27.0 %all-to-all-start.1 = ((bf16[128,16,128]{2,1,0:T(8,128)(2,1)}), bf16[128,16,128]{2,1,0:T(8,128)(2,1)S(1)}, u32[]{:S(2)}, u32[]{:S(2)}) async-start(bf16[128,16,128]{2,1,0:T(8,128)(2,1)} %bitcast.2), calls=%async_computation.1 | async-start | bytes 1048576 | tf_op jit(solution)/shard_map/all_to_all | solution.py:301
  64.6 0.7 copy-start.4
  64.6 1.0 %copy-start.5 = (f32[2048]{0:T(1024)S(1)}, f32[2048]{0:T(1024)}, u32[]{:S(2)}) copy-start(f32[2048]{0:T(1024)} %param.9) | copy-start | bytes 24580

commit v7 on v6

--- a/solution.py
+++ b/solution.py
@@ -229,7 +229,7 @@
     return tuple(pltpu.with_memory_space_constraint(x, pltpu.VMEM) for x in arrays)
 
 
-def gate(back, query, direct, gain):
+def gate(back, query, direct, gain, copies):
     chan, length = query.shape
     chunk = chan // 4
 
@@ -241,12 +241,12 @@
             gated = (query_ref[rows, :].astype(f32) * mixed).astype(bf16).astype(f32)
             out_ref[rows, :] = gated * gain_ref[rows, :]
             total = total + jnp.sum((gated * gated).reshape(chunk // 8, 8, length), axis=0)
-        sum_ref[...] = jnp.sum(total, axis=0, keepdims=True)
+        sum_ref[...] = jnp.broadcast_to(jnp.sum(total, axis=0, keepdims=True), (copies, 1, length))
 
     whole = pl.BlockSpec(memory_space=pltpu.VMEM)
     return pl.pallas_call(
         kernel,
-        out_shape=(pltpu.VMEM((chan, length), f32), pltpu.VMEM((1, length), f32)),
+        out_shape=(pltpu.VMEM((chan, length), f32), pltpu.VMEM((copies, 1, length), f32)),
         in_specs=[whole] * 4,
         out_specs=(whole, whole),
         compiler_params=pltpu.CompilerParams(vmem_limit_bytes=16 << 20),
@@ -307,8 +307,8 @@
     gain, product = lax.optimization_barrier((gain, product))
     direct = skip_gain[:, None] * product.astype(f32)
     direct, gain, query, back = lax.optimization_barrier((direct, gain, query, back))
-    gated, squares = gate(back, query, direct, gain)
-    return finish(gated, lax.all_gather(squares, "tp"), local_chan * n_width)
+    gated, squares = gate(back, query, direct, gain, n_width)
+    return finish(gated, lax.all_to_all(squares, "tp", 0, 0), local_chan * n_width)
 
 
 def solution(mesh):

time: 87.3 us -> 87.1 us (level)
    all_gather x1 -> x0, blocking collectives: 9.67 us -> none  [shards(): return finish(gated, lax.all_gather(squares, 'tp'), local_chan * n_width)]
    all_to_all x0 -> x1, blocking collectives: none -> 9.35 us  [shards(): lax.all_to_all(squares, 'tp', 0, 0)]
where the time goes in v7:
time: 87.1 us; the launch traced here: 86.7 us
  waiting for transfers between devices  26.9 us (31%)
  starting transfers between devices  26.1 us (30%)
  Pallas kernels  11.1 us (13%)
  blocking collectives  9.35 us (11%)
  other arithmetic  7.65 us (9%)
  local copies, waits for them, and re-layouts  5.29 us (6%)
    all_to_all x1, starting transfers between devices, shards(): recv = lax.all_to_all(send, 'ctx', 0, 0)  17.4 us
    all_to_all x1, waiting for transfers between devices, shards(): recv = lax.all_to_all(send, 'ctx', 0, 0)  16.9 us
    all_to_all x1, waiting for transfers between devices, shards(): back = lax.all_to_all(mixed, 'ctx', 0, 0).reshape(local_chan, length)  10 us
    all_to_all x1, blocking collectives, shards(): lax.all_to_all(squares, 'tp', 0, 0)  9.35 us
    all_to_all x1, starting transfers between devices, shards(): back = lax.all_to_all(mixed, 'ctx', 0, 0).reshape(local_chan, length)  6.67 us
    pallas_call x1, Pallas kernels, long_conv_blocks(): pl.pallas_call(kernel, out_shape=jax.ShapeDtypeStruct((half, 2, owned, LA...  6.14 us
    add x1, other arithmetic, local_streams(): conv + short_weight[offset][:, :, None] * padded[:, :, start:start + length]  4.67 us
    pallas_call x1, Pallas kernels, pack_product(): pl.pallas_call(kernel, out_shape=jax.ShapeDtypeStruct(packed, bf16), in_s...  3.76 us
  transfers between devices with their start and end apart: 3, of which 2 were waited for; matrix products, arithmetic and copies ran while one was open for 14% of the time, Pallas kernels for 7%

profile of v7, /device:TPU:8, one launch (start us, length us, event | category | flops | bytes accessed | tf_op | source)
XLA Modules:
  0.0 86.7 jit_solution(5597761970879698501)
XLA Ops:
  0.0 0.0 copy-start
  0.0 0.0 copy-start.1
  0.0 3.8 %pack_product.1 = bf16[128,9,2,128]{3,2,1,0:T(2,128)(2,1)} custom-call(bf16[3,2048,128]{2,1,0:T(8,128)(2,1)} %streams_in.1, f32[3,3,2048]{2,1,0:T(4,128)} %weight_in.1, f32[128,128]{1,0:T(8,128)} %filt_in.1), custom_call_target="tpu_custom_call" | custom-call | tf_op jit(solution)/shard_map/pack_product/pallas_call | solution.py:93
  3.8 17.4 %all-to-all-start = ((bf16[128,9,2,128]{3,2,1,0:T(2,128)(2,1)}), bf16[128,9,2,128]{3,2,1,0:T(2,128)(2,1)S(1)}, u32[]{:S(2)}, u32[]{:S(2)}) async-start(bf16[128,9,2,128]{3,2,1,0:T(2,128)(2,1)} %pack_product.1), calls=%async_computation | async-start | bytes 1179648 | tf_op jit(solution)/shard_map/all_to_all | solution.py:294
  21.2 0.0 copy-done.1
  21.2 1.6 %copy.9 = bf16[3,2048,128]{1,2,0:T(8,128)(2,1)} copy(bf16[3,2048,128]{2,1,0:T(8,128)(2,1)S(1)} %copy-done.1) | data formatting | bytes 3145728 | tf_op jit(solution)/shard_map/optimization_barrier | solution.py:295
  22.8 0.9 %slice.45 = bf16[3,2048,2]{1,2,0:T(2,128)(2,1)S(1)} slice(bf16[3,2048,128]{1,2,0:T(8,128)(2,1)} %copy.9), slice={[0:3], [0:2048], [126:128]} | slice | bytes 49152 | tf_op jit(solution)/shard_map/slice | solution.py:299
  23.7 2.1 %collective-permute-start = (bf16[3,2048,2]{1,2,0:T(2,128)(2,1)S(1)}, bf16[3,2048,2]{1,2,0:T(2,128)(2,1)S(1)}, u32[]{:S(2)}, u32[]{:S(2)}) collective-permute-start(bf16[3,2048,2]{1,2,0:T(2,128)(2,1)S(1)} %slice.45), channel_id=1, source_target_pairs={{0,4},{4,8},{8,12},{12,16},{16,20},{20,24},{24,28},{28,32},{32,36}... | collective-permute-start | bytes 73736 | tf_op jit(solution)/shard_map/ppermute | solution.py:299
  25.8 0.0 copy-done.3
  25.8 0.1 dynamic-slice_bitcast_fusion
  25.9 0.1 tile.12
  26.0 16.9 %all-to-all-done = bf16[128,9,2,128]{3,2,1,0:T(2,128)(2,1)S(1)} async-done(((bf16[128,9,2,128]{3,2,1,0:T(2,128)(2,1)}), bf16[128,9,2,128]{3,2,1,0:T(2,128)(2,1)S(1)}, u32[]{:S(2)}, u32[]{:S(2)}) %all-to-all-start) | async-done | bytes 589856 | tf_op jit(solution)/shard_map/all_to_all | solution.py:294
  42.9 0.0 copy-done
  42.9 6.1 %long_conv.1 = bf16[64,2,16,128]{3,2,1,0:T(8,128)(2,1)} custom-call(bf16[64,2,9,2,128]{4,3,2,1,0:T(2,128)(2,1)S(1)} %bitcast.15, f32[8,128]{1,0:T(8,128)S(1)} %pad.4.weight_ref, bf16[256,768]{1,0:T(8,128)(2,1)S(1)} %copy-done), custom_call_target="tpu_custom_call" | custom-call | tf_op jit(solution)/shard_map/long_conv/pallas_call | solution.py:199
  49.0 6.7 %all-to-all-start.1 = ((bf16[128,16,128]{2,1,0:T(8,128)(2,1)}), bf16[128,16,128]{2,1,0:T(8,128)(2,1)S(1)}, u32[]{:S(2)}, u32[]{:S(2)}) async-start(bf16[128,16,128]{2,1,0:T(8,128)(2,1)} %bitcast.2), calls=%async_computation.1 | async-start | bytes 1048576 | tf_op jit(solution)/shard_map/all_to_all | solution.py:301
  55.7 0.0 collective-permute-done
  55.7 1.6 %copy.11 = bf16[3,2048,2]{2,1,0:T(8,128)(2,1)} copy(bf16[3,2048,2]{1,2,0:T(2,128)(2,1)S(1)} %collective-permute-done) | data formatting | bytes 49152 | tf_op jit(solution)/shard_map/optimization_barrier | solution.py:302
  57.3 0.0 copy-done.2
  57.4 2.5 %maximum_convert_fusion = f32[3,2048,130]{2,1,0:T(8,128)S(1)} fusion(bf16[3,2048,128]{2,1,0:T(8,128)(2,1)S(1)} %copy-done.2, bf16[3,2048,2]{2,1,0:T(8,128)(2,1)} %copy.11), kind=kLoop, calls=%fused_computation.5 | loop fusion | flops 3194880 | bytes 4792320 | tf_op jit(solution)/shard_map/convert_element_type | solution.py:220
  59.9 4.7 %fusion = f32[3,2048,128]{2,1,0:T(8,128)S(1)} fusion(f32[3,2048,130]{2,1,0:T(8,128)S(1)} %maximum_convert_fusion, f32[3,2048]{1,0:T(4,128)S(1)} %get-tuple-element.40, f32[3,2048]{1,0:T(4,128)S(1)} %get-tuple-element.41, f32[3,2048]{1,0:T(4,128)S(1)} %get-tuple-element.39), kind=kLoop, calls=%fused_computation.1 | loop fusion | flops 3932160 | bytes 12656640 | tf_op jit(solution)/shard_map/add | solution.py:224
  64.6 0.0 copy-start.4
  64.6 0.0 copy-start.5
  64.6 0.1 fusion.3.query_ref
  64.7 0.1 fusion.4
  64.8 0.5 copy-done.4
  65.3 0.3 broadcast_in_dim.2.gain_ref
  65.6 0.0 copy-done.5
  65.6 0.3 convert_multiply_fusion.direct_ref
  66.0 10.0 %all-to-all-done.1 = bf16[128,16,128]{2,1,0:T(8,128)(2,1)S(1)} async-done(((bf16[128,16,128]{2,1,0:T(8,128)(2,1)}), bf16[128,16,128]{2,1,0:T(8,128)(2,1)S(1)}, u32[]{:S(2)}, u32[]{:S(2)}) %all-to-all-start.1) | async-done | bytes 524320 | tf_op jit(solution)/shard_map/all_to_all | solution.py:301
  76.0 0.3 gate.1
  76.3 9.3 %all_to_all.15.squares_ref = f32[4,1,128]{2,1,0:T(1,128)S(1)} all-to-all(f32[4,1,128]{2,1,0:T(1,128)S(1)} %get-tuple-element.38), channel_id=1, replica_groups=mesh['ctx'=128,'tp'=4] {'tp'}, dimensions={0} | all-to-all | bytes 4096 | tf_op jit(solution)/shard_map/all_to_all | solution.py:311
  85.7 0.9 finish.1
  (7 shorter events, 0.1 us)
Async XLA Ops:
  0.0 42.9 %copy-start = (bf16[256,768]{1,0:T(8,128)(2,1)S(1)}, bf16[256,768]{1,0:T(8,128)(2,1)}, u32[]{:S(2)}) copy-start(bf16[256,768]{1,0:T(8,128)(2,1)} %constant.16.clone.terms_ref) | copy-start | bytes 1179652
  0.0 21.2 %copy-start.1 = (bf16[3,2048,128]{2,1,0:T(8,128)(2,1)S(1)}, bf16[3,2048,128]{2,1,0:T(8,128)(2,1)}, u32[]{:S(2)}) copy-start(bf16[3,2048,128]{2,1,0:T(8,128)(2,1)} %streams_in.1) | copy-start | bytes 4718596
  0.0 25.8 %copy-start.3 = (f32[3,3,2048]{2,1,0:T(4,128)S(1)}, f32[3,3,2048]{2,1,0:T(4,128)}, u32[]{:S(2)}) copy-start(f32[3,3,2048]{2,1,0:T(4,128)} %weight_in.1) | copy-start | bytes 221188
  3.8 39.1 %all-to-all-start = ((bf16[128,9,2,128]{3,2,1,0:T(2,128)(2,1)}), bf16[128,9,2,128]{3,2,1,0:T(2,128)(2,1)S(1)}, u32[]{:S(2)}, u32[]{:S(2)}) async-start(bf16[128,9,2,128]{3,2,1,0:T(2,128)(2,1)} %pack_product.1), calls=%async_computation | async-start | bytes 1179648 | tf_op jit(solution)/shard_map/all_to_all | solution.py:294
  23.7 31.9 %collective-permute-start = (bf16[3,2048,2]{1,2,0:T(2,128)(2,1)S(1)}, bf16[3,2048,2]{1,2,0:T(2,128)(2,1)S(1)}, u32[]{:S(2)}, u32[]{:S(2)}) collective-permute-start(bf16[3,2048,2]{1,2,0:T(2,128)(2,1)S(1)} %slice.45), channel_id=1, source_target_pairs={{0,4},{4,8},{8,12},{12,16},{16,20},{20,24},{24,28},{28,32},{32,36}... | collective-permute-start | bytes 73736 | tf_op jit(solution)/shard_map/ppermute | solution.py:299
  49.0 8.3 %copy-start.2 = (bf16[3,2048,128]{2,1,0:T(8,128)(2,1)S(1)}, bf16[3,2048,128]{2,1,0:T(8,128)(2,1)}, u32[]{:S(2)}) copy-start(bf16[3,2048,128]{2,1,0:T(8,128)(2,1)} %streams_in.1) | copy-start | bytes 4718596
  49.0 27.0 %all-to-all-start.1 = ((bf16[128,16,128]{2,1,0:T(8,128)(2,1)}), bf16[128,16,128]{2,1,0:T(8,128)(2,1)S(1)}, u32[]{:S(2)}, u32[]{:S(2)}) async-start(bf16[128,16,128]{2,1,0:T(8,128)(2,1)} %bitcast.2), calls=%async_computation.1 | async-start | bytes 1048576 | tf_op jit(solution)/shard_map/all_to_all | solution.py:301
  64.6 0.7 copy-start.4
  64.6 1.0 %copy-start.5 = (f32[2048]{0:T(1024)S(1)}, f32[2048]{0:T(1024)}, u32[]{:S(2)}) copy-start(f32[2048]{0:T(1024)} %param.9) | copy-start | bytes 24580

commit v8 on v6

--- a/solution.py
+++ b/solution.py
@@ -257,7 +257,7 @@
 def finish(gated, squares, count):
     chan, length = gated.shape
 
-    parts = 2
+    parts = 1
     chunk = chan // parts
 
     def kernel(gated_ref, squares_ref, out_ref, done_ref, sems):

time: 87.3 us -> 87.4 us (level)
  no operation moved by 1% of the time
where the time goes in v8:
time: 87.4 us; the launch traced here: 87 us
  waiting for transfers between devices  26.9 us (31%)
  starting transfers between devices  26.1 us (30%)
  Pallas kernels  11.1 us (13%)
  blocking collectives  9.67 us (11%)
  other arithmetic  7.65 us (9%)
  local copies, waits for them, and re-layouts  5.29 us (6%)
    all_to_all x1, starting transfers between devices, shards(): recv = lax.all_to_all(send, 'ctx', 0, 0)  17.4 us
    all_to_all x1, waiting for transfers between devices, shards(): recv = lax.all_to_all(send, 'ctx', 0, 0)  16.9 us
    all_to_all x1, waiting for transfers between devices, shards(): back = lax.all_to_all(mixed, 'ctx', 0, 0).reshape(local_chan, length)  10 us
    all_gather x1, blocking collectives, shards(): return finish(gated, lax.all_gather(squares, 'tp'), local_chan * n_width)  9.67 us
    all_to_all x1, starting transfers between devices, shards(): back = lax.all_to_all(mixed, 'ctx', 0, 0).reshape(local_chan, length)  6.67 us
    pallas_call x1, Pallas kernels, long_conv_blocks(): pl.pallas_call(kernel, out_shape=jax.ShapeDtypeStruct((half, 2, owned, LA...  6.14 us
    add x1, other arithmetic, local_streams(): conv + short_weight[offset][:, :, None] * padded[:, :, start:start + length]  4.67 us
    pallas_call x1, Pallas kernels, pack_product(): pl.pallas_call(kernel, out_shape=jax.ShapeDtypeStruct(packed, bf16), in_s...  3.76 us
  transfers between devices with their start and end apart: 3, of which 2 were waited for; matrix products, arithmetic and copies ran while one was open for 14% of the time, Pallas kernels for 7%

profile of v8, /device:TPU:8, one launch (start us, length us, event | category | flops | bytes accessed | tf_op | source)
XLA Modules:
  0.0 87.0 jit_solution(13369808243924694735)
XLA Ops:
  0.0 0.0 copy-start
  0.0 0.0 copy-start.1
  0.0 3.8 %pack_product.1 = bf16[128,9,2,128]{3,2,1,0:T(2,128)(2,1)} custom-call(bf16[3,2048,128]{2,1,0:T(8,128)(2,1)} %streams_in.1, f32[3,3,2048]{2,1,0:T(4,128)} %weight_in.1, f32[128,128]{1,0:T(8,128)} %filt_in.1), custom_call_target="tpu_custom_call" | custom-call | tf_op jit(solution)/shard_map/pack_product/pallas_call | solution.py:93
  3.8 17.4 %all-to-all-start = ((bf16[128,9,2,128]{3,2,1,0:T(2,128)(2,1)}), bf16[128,9,2,128]{3,2,1,0:T(2,128)(2,1)S(1)}, u32[]{:S(2)}, u32[]{:S(2)}) async-start(bf16[128,9,2,128]{3,2,1,0:T(2,128)(2,1)} %pack_product.1), calls=%async_computation | async-start | bytes 1179648 | tf_op jit(solution)/shard_map/all_to_all | solution.py:294
  21.2 0.0 copy-done.1
  21.2 1.6 %copy.9 = bf16[3,2048,128]{1,2,0:T(8,128)(2,1)} copy(bf16[3,2048,128]{2,1,0:T(8,128)(2,1)S(1)} %copy-done.1) | data formatting | bytes 3145728 | tf_op jit(solution)/shard_map/optimization_barrier | solution.py:295
  22.8 0.9 %slice.45 = bf16[3,2048,2]{1,2,0:T(2,128)(2,1)S(1)} slice(bf16[3,2048,128]{1,2,0:T(8,128)(2,1)} %copy.9), slice={[0:3], [0:2048], [126:128]} | slice | bytes 49152 | tf_op jit(solution)/shard_map/slice | solution.py:299
  23.7 2.1 %collective-permute-start = (bf16[3,2048,2]{1,2,0:T(2,128)(2,1)S(1)}, bf16[3,2048,2]{1,2,0:T(2,128)(2,1)S(1)}, u32[]{:S(2)}, u32[]{:S(2)}) collective-permute-start(bf16[3,2048,2]{1,2,0:T(2,128)(2,1)S(1)} %slice.45), channel_id=1, source_target_pairs={{0,4},{4,8},{8,12},{12,16},{16,20},{20,24},{24,28},{28,32},{32,36}... | collective-permute-start | bytes 73736 | tf_op jit(solution)/shard_map/ppermute | solution.py:299
  25.8 0.0 copy-done.3
  25.8 0.1 dynamic-slice_bitcast_fusion
  25.9 0.1 tile.12
  26.0 16.9 %all-to-all-done = bf16[128,9,2,128]{3,2,1,0:T(2,128)(2,1)S(1)} async-done(((bf16[128,9,2,128]{3,2,1,0:T(2,128)(2,1)}), bf16[128,9,2,128]{3,2,1,0:T(2,128)(2,1)S(1)}, u32[]{:S(2)}, u32[]{:S(2)}) %all-to-all-start) | async-done | bytes 589856 | tf_op jit(solution)/shard_map/all_to_all | solution.py:294
  42.9 0.0 copy-done
  42.9 6.1 %long_conv.1 = bf16[64,2,16,128]{3,2,1,0:T(8,128)(2,1)} custom-call(bf16[64,2,9,2,128]{4,3,2,1,0:T(2,128)(2,1)S(1)} %bitcast.16, f32[8,128]{1,0:T(8,128)S(1)} %pad.4.weight_ref, bf16[256,768]{1,0:T(8,128)(2,1)S(1)} %copy-done), custom_call_target="tpu_custom_call" | custom-call | tf_op jit(solution)/shard_map/long_conv/pallas_call | solution.py:199
  49.0 6.7 %all-to-all-start.1 = ((bf16[128,16,128]{2,1,0:T(8,128)(2,1)}), bf16[128,16,128]{2,1,0:T(8,128)(2,1)S(1)}, u32[]{:S(2)}, u32[]{:S(2)}) async-start(bf16[128,16,128]{2,1,0:T(8,128)(2,1)} %bitcast.2), calls=%async_computation.1 | async-start | bytes 1048576 | tf_op jit(solution)/shard_map/all_to_all | solution.py:301
  55.7 0.0 collective-permute-done
  55.7 1.6 %copy.11 = bf16[3,2048,2]{2,1,0:T(8,128)(2,1)} copy(bf16[3,2048,2]{1,2,0:T(2,128)(2,1)S(1)} %collective-permute-done) | data formatting | bytes 49152 | tf_op jit(solution)/shard_map/optimization_barrier | solution.py:302
  57.3 0.0 copy-done.2
  57.4 2.5 %maximum_convert_fusion = f32[3,2048,130]{2,1,0:T(8,128)S(1)} fusion(bf16[3,2048,128]{2,1,0:T(8,128)(2,1)S(1)} %copy-done.2, bf16[3,2048,2]{2,1,0:T(8,128)(2,1)} %copy.11), kind=kLoop, calls=%fused_computation.5 | loop fusion | flops 3194880 | bytes 4792320 | tf_op jit(solution)/shard_map/convert_element_type | solution.py:220
  59.9 4.7 %fusion = f32[3,2048,128]{2,1,0:T(8,128)S(1)} fusion(f32[3,2048,130]{2,1,0:T(8,128)S(1)} %maximum_convert_fusion, f32[3,2048]{1,0:T(4,128)S(1)} %get-tuple-element.40, f32[3,2048]{1,0:T(4,128)S(1)} %get-tuple-element.41, f32[3,2048]{1,0:T(4,128)S(1)} %get-tuple-element.39), kind=kLoop, calls=%fused_computation.1 | loop fusion | flops 3932160 | bytes 12656640 | tf_op jit(solution)/shard_map/add | solution.py:224
  64.6 0.0 copy-start.4
  64.6 0.0 copy-start.5
  64.6 0.1 fusion.3.query_ref
  64.7 0.1 fusion.4
  64.8 0.5 copy-done.4
  65.3 0.3 broadcast_in_dim.2.gain_ref
  65.6 0.0 copy-done.5
  65.6 0.3 convert_multiply_fusion.direct_ref
  66.0 10.0 %all-to-all-done.1 = bf16[128,16,128]{2,1,0:T(8,128)(2,1)S(1)} async-done(((bf16[128,16,128]{2,1,0:T(8,128)(2,1)}), bf16[128,16,128]{2,1,0:T(8,128)(2,1)S(1)}, u32[]{:S(2)}, u32[]{:S(2)}) %all-to-all-start.1) | async-done | bytes 524320 | tf_op jit(solution)/shard_map/all_to_all | solution.py:301
  76.0 0.3 gate.1
  76.3 9.7 %all-gather.1.squares_ref = f32[4,1,128]{2,1,0:T(1,128)S(1)} all-gather(f32[1,1,128]{2,1,0:T(1,128)S(1)} %bitcast.18), channel_id=2, replica_groups=mesh['ctx'=128,'tp'=4] {'tp'}, dimensions={0}, use_global_device_ids=true | all-gather | bytes 2560 | tf_op jit(solution)/shard_map/all_gather | solution.py:311
  86.0 0.9 %finish.1 = bf16[2048,128]{1,0:T(8,128)(2,1)} custom-call(f32[2048,128]{1,0:T(8,128)S(1)} %get-tuple-element.37.gated_ref, f32[4,1,128]{2,1,0:T(1,128)S(1)} %all-gather.1.squares_ref), custom_call_target="tpu_custom_call" | custom-call | tf_op jit(solution)/shard_map/finish/pallas_call | solution.py:275
  (7 shorter events, 0.1 us)
Async XLA Ops:
  0.0 42.9 %copy-start = (bf16[256,768]{1,0:T(8,128)(2,1)S(1)}, bf16[256,768]{1,0:T(8,128)(2,1)}, u32[]{:S(2)}) copy-start(bf16[256,768]{1,0:T(8,128)(2,1)} %constant.16.clone.terms_ref) | copy-start | bytes 1179652
  0.0 21.2 %copy-start.1 = (bf16[3,2048,128]{2,1,0:T(8,128)(2,1)S(1)}, bf16[3,2048,128]{2,1,0:T(8,128)(2,1)}, u32[]{:S(2)}) copy-start(bf16[3,2048,128]{2,1,0:T(8,128)(2,1)} %streams_in.1) | copy-start | bytes 4718596
  0.0 25.8 %copy-start.3 = (f32[3,3,2048]{2,1,0:T(4,128)S(1)}, f32[3,3,2048]{2,1,0:T(4,128)}, u32[]{:S(2)}) copy-start(f32[3,3,2048]{2,1,0:T(4,128)} %weight_in.1) | copy-start | bytes 221188
  3.8 39.1 %all-to-all-start = ((bf16[128,9,2,128]{3,2,1,0:T(2,128)(2,1)}), bf16[128,9,2,128]{3,2,1,0:T(2,128)(2,1)S(1)}, u32[]{:S(2)}, u32[]{:S(2)}) async-start(bf16[128,9,2,128]{3,2,1,0:T(2,128)(2,1)} %pack_product.1), calls=%async_computation | async-start | bytes 1179648 | tf_op jit(solution)/shard_map/all_to_all | solution.py:294
  23.7 31.9 %collective-permute-start = (bf16[3,2048,2]{1,2,0:T(2,128)(2,1)S(1)}, bf16[3,2048,2]{1,2,0:T(2,128)(2,1)S(1)}, u32[]{:S(2)}, u32[]{:S(2)}) collective-permute-start(bf16[3,2048,2]{1,2,0:T(2,128)(2,1)S(1)} %slice.45), channel_id=1, source_target_pairs={{0,4},{4,8},{8,12},{12,16},{16,20},{20,24},{24,28},{28,32},{32,36}... | collective-permute-start | bytes 73736 | tf_op jit(solution)/shard_map/ppermute | solution.py:299
  49.0 8.3 %copy-start.2 = (bf16[3,2048,128]{2,1,0:T(8,128)(2,1)S(1)}, bf16[3,2048,128]{2,1,0:T(8,128)(2,1)}, u32[]{:S(2)}) copy-start(bf16[3,2048,128]{2,1,0:T(8,128)(2,1)} %streams_in.1) | copy-start | bytes 4718596
  49.0 27.0 %all-to-all-start.1 = ((bf16[128,16,128]{2,1,0:T(8,128)(2,1)}), bf16[128,16,128]{2,1,0:T(8,128)(2,1)S(1)}, u32[]{:S(2)}, u32[]{:S(2)}) async-start(bf16[128,16,128]{2,1,0:T(8,128)(2,1)} %bitcast.2), calls=%async_computation.1 | async-start | bytes 1048576 | tf_op jit(solution)/shard_map/all_to_all | solution.py:301
  64.6 0.7 copy-start.4
  64.6 1.0 %copy-start.5 = (f32[2048]{0:T(1024)S(1)}, f32[2048]{0:T(1024)}, u32[]{:S(2)}) copy-start(f32[2048]{0:T(1024)} %param.9) | copy-start | bytes 24580
